TPU v7x, 128 devices: a whole 4x4x4 slice. The times are simulated.
128 devices in a mesh: dp: 2 (over core), expert: 64 (over y, x, z).
Axes of the slice: x: 4, y: 4, z: 4, core: 2. Of those that a mesh axis runs over, the one named last changes fastest.
Arguments:
- tokens: bfloat16 [8192, 2048], P(('dp', 'expert')), may hold values from -6 to 6
- tangent: bfloat16 [8192, 2048], P(('dp', 'expert'))
- adjoint: bfloat16 [8192, 2048], P(('dp', 'expert')), may hold values from -6 to 6
- gates: float32 [8192, 8], P(('dp', 'expert')), may hold values from 0.05 to 0.5
- expert_ids: int32 [8192, 8], P(('dp', 'expert')), may hold values from 0 to 127, all different within a row; in each aligned block of 64 rows (0 to 63, 64 to 127, ...) at most 8 rows name the same one
- w_gate: bfloat16 [128, 2048, 768], P('expert'), may hold values from -0.125 to 0.125
- w_up: bfloat16 [128, 2048, 768], P('expert'), may hold values from -0.125 to 0.125
- w_down: bfloat16 [128, 768, 2048], P('expert'), may hold values from -0.21875 to 0.21875
Outputs:
- hvp: float32 [8192, 2048], P(('dp', 'expert'))
- quotient: float32 [], replicated
Inputs may be any that keep to these rules, and one draw needn't show every extreme that they name: `expert_ids`: each token names 8 different experts. Among the tokens of one device no expert is named more than 8 times, a bound that some block reaches; every expert is named somewhere.
All inputs are finite; a program needn't handle non-finite values.
Results may differ from a plain program's by a relative error of at most 0.0041.
Values may be sent and summed in bfloat16 or wider, within the bound.
A program may use at most 128 MiB of HBM per device.

v0:
```python
import functools

import jax
import jax.numpy as jnp
from jax import lax
from jax.experimental import pallas as pl
from jax.experimental.pallas import tpu as pltpu
from jax.sharding import PartitionSpec as P

MESH = pl.DeviceIdType.MESH
STRIDE = (16, 4, 1)
ORDERS = ((0, 1, 2), (1, 2, 0), (2, 0, 1))
PARTS = ((0, 768), (768, 640), (1408, 640))
TOK, D, FF, R = 64, 2048, 768, 4
BF, F32 = jnp.bfloat16, jnp.float32


class Place:
    def __init__(self):
        self.me = lax.axis_index("expert")
        self.dp = lax.axis_index("dp")
        self.at = (self.me // 16, (self.me // 4) % 4, self.me % 4)

    def shifted(self, dim, by):
        c = self.at[dim]
        return self.me + (lax.rem(c + by, 4) - c) * STRIDE[dim]


def barrier(place, core):
    sem = pltpu.get_barrier_semaphore()
    for dim in range(3):
        for by in (1, 2, 3):
            pl.semaphore_signal(
                sem, inc=1, device_id=(place.dp, place.shifted(dim, by)), device_id_type=MESH
            )
    if core:
        pl.semaphore_signal(sem, inc=1, device_id=(1 - place.dp, place.me), device_id_type=MESH)
    pl.semaphore_wait(sem, 10 if core else 9)


class Wire:
    def __init__(self, place, send, recv):
        self.place, self.send, self.recv, self.used, self.open = place, send, recv, 0, []

    def take(self):
        self.used += 1
        return self.used - 1

    def _copy(self, src, dst, k, target):
        return pltpu.make_async_remote_copy(
            src_ref=src, dst_ref=dst, send_sem=self.send.at[k], recv_sem=self.recv.at[k],
            device_id=target, device_id_type=MESH,
        )

    def go(self, k, src, dst, dim, by):
        c = self._copy(src, dst, k, (self.place.dp, self.place.shifted(dim, by)))
        c.start()
        self.open.append(c)

    def cross(self, k, src, dst):
        c = self._copy(src, dst, k, (1 - self.place.dp, self.place.me))
        c.start()
        self.open.append(c)

    def got(self, k, view):
        self._copy(view, view, k, (self.place.dp, self.place.shifted(0, 1))).wait_recv()

    def drain(self):
        for c in self.open:
            c.wait_send()
        self.open = []


def mod4(v):
    return lax.rem(v, 4)


def column_terms(meta, a, s2, place):
    dim = ORDERS[a][2]
    blocks = [meta[a, s2, s] for s in range(4)]
    low = lax.broadcasted_iota(jnp.int32, (8, 128), 1) < 64
    turn = [pltpu.roll(b, 64, 1) for b in blocks]
    ids = jnp.concatenate([jnp.where(low, blocks[0], turn[1]), jnp.where(low, blocks[2], turn[3])], axis=1)
    gates = jnp.concatenate([jnp.where(low, turn[0], blocks[1]), jnp.where(low, turn[2], blocks[3])], axis=1)
    row = lax.broadcasted_iota(jnp.int32, (8, 256), 0)
    named = jnp.zeros((8, 256), F32)
    weight = jnp.zeros((8, 256), F32)
    for r in range(8):
        e = 2 * (place.me + (r // 2 - place.at[dim]) * STRIDE[dim]) + r % 2
        hit = ids == e.astype(F32)
        n = jnp.sum(jnp.where(hit, 1.0, 0.0), axis=0, keepdims=True)
        g = jnp.sum(jnp.where(hit, gates, 0.0), axis=0, keepdims=True)
        named = jnp.where(row == r, n, named)
        weight = jnp.where(row == r, g, weight)
    i = lax.broadcasted_iota(jnp.int32, (256, 256), 0)
    l = lax.broadcasted_iota(jnp.int32, (256, 256), 1)
    upper = jnp.where((i // 64 == l // 64) & (i < l), 1.0, 0.0).astype(BF)
    before = jnp.dot(named.astype(BF), upper, preferred_element_type=F32)
    base = (lax.broadcasted_iota(jnp.int32, (8, 256), 1) // 64 * 8).astype(F32)
    return jnp.where(named > 0.5, base + before, -1.0), weight


def dispatch_kernel(tok, tan, adj, meta_in, r0, r1, r2, meta_out,
                    held, packed, relay, meta, pick, send, recv, local):
    place = Place()
    wire = Wire(place, send, recv)
    outs = (r0, r1, r2)
    barrier(place, False)

    own = []
    for a, src in enumerate((tok, tan, adj)):
        d1, d2, d3 = ORDERS[a]
        c = pltpu.make_async_copy(src, held.at[a, place.at[d2], place.at[d1]], local.at[a])
        c.start()
        own.append(c)
        c = pltpu.make_async_copy(meta_in, meta.at[a, place.at[d2], place.at[d1]], local.at[3 + a])
        c.start()
        own.append(c)
    for c in own:
        c.wait()

    def half(a, s2, s1, h):
        return held.at[a, s2, s1, pl.ds(32 * h, 32)]

    def spread(a, dim, at2, at1, keys):
        for h in (0, 1):
            wire.go(keys[0][h], half(a, at2, at1, h), half(a, at2, at1, h), dim, 1)
            wire.go(keys[1][1 - h], half(a, at2, at1, 1 - h), half(a, at2, at1, 1 - h), dim, 3)

    def keys_of():
        return ((wire.take(), wire.take()), (wire.take(), wire.take()), (wire.take(), wire.take()))

    first = [keys_of() for _ in range(3)]
    second = [[keys_of() for _ in range(4)] for _ in range(3)]
    rel1 = (0, 3, 1, 2)
    at = [(place.at[ORDERS[a][1]], place.at[ORDERS[a][0]]) for a in range(3)]

    mk1 = [[wire.take() for _ in range(3)] for _ in range(3)]
    mk2 = [[wire.take() for _ in range(3)] for _ in range(3)]
    for a in range(3):
        n2, n1 = at[a]
        for i, by in enumerate((1, 2, 3)):
            wire.go(mk1[a][i], meta.at[a, n2, n1], meta.at[a, n2, n1], ORDERS[a][0], by)
    for a in range(3):
        n2, n1 = at[a]
        spread(a, ORDERS[a][0], n2, n1, first[a])
    for a in range(3):
        n2, n1 = at[a]
        spread(a, ORDERS[a][1], n2, n1, second[a][0])
    for a in range(3):
        n2, n1 = at[a]
        for i, by in enumerate((1, 2, 3)):
            wire.got(mk1[a][i], meta.at[a, n2, mod4(n1 + 4 - by)])
        for i, by in enumerate((1, 2, 3)):
            wire.go(mk2[a][i], meta.at[a, n2], meta.at[a, n2], ORDERS[a][1], by)

    def pass_on(a, dim, keys, minus, plus):
        wire.got(keys[0][0], minus(0))
        wire.go(keys[2][0], minus(0), minus(0), dim, 1)
        wire.got(keys[1][1], plus(1))
        wire.go(keys[2][1], plus(1), plus(1), dim, 3)

    def rest(keys, minus, plus):
        wire.got(keys[0][1], minus(1))
        wire.got(keys[1][0], plus(0))

    def views1(a):
        n2, n1 = at[a]
        return (lambda h: half(a, n2, mod4(n1 + 3), h)), (lambda h: half(a, n2, mod4(n1 + 1), h))

    def views2(a, b):
        n2, n1 = at[a]
        s1 = mod4(n1 + rel1[b])
        return (lambda h: half(a, mod4(n2 + 3), s1, h)), (lambda h: half(a, mod4(n2 + 1), s1, h))

    for a in range(3):
        pass_on(a, ORDERS[a][0], first[a], *views1(a))
    for a in range(3):
        rest(first[a], *views1(a))
        n2, n1 = at[a]
        for b in (1, 2):
            spread(a, ORDERS[a][1], n2, mod4(n1 + rel1[b]), second[a][b])
    for a in range(3):
        pass_on(a, ORDERS[a][1], second[a][0], *views2(a, 0))
    for a in range(3):
        n2, n1 = at[a]
        wire.got(first[a][2][0], half(a, n2, mod4(n1 + 2), 0))
        wire.got(first[a][2][1], half(a, n2, mod4(n1 + 2), 1))
        spread(a, ORDERS[a][1], n2, mod4(n1 + 2), second[a][3])

    moved = []
    third = [[[wire.take() for _ in range(6)] for _ in range(4)] for _ in range(3)]

    def pack(a, r):
        n2, n1 = at[a]
        dim = ORDERS[a][2]
        n3 = place.at[dim]
        s2 = mod4(n2 + r)
        index, _ = column_terms(meta, a, s2, place)
        slots = lax.broadcasted_iota(jnp.int32, (32, 256), 0).astype(F32)
        for e in range(8):
            pick[pl.ds(32 * e, 32), :] = jnp.where(index[e : e + 1, :] == slots, 1.0, 0.0).astype(BF)
        chosen = pick[...]

        @pl.loop(0, 4)
        def _(n):
            cols = pl.ds(pl.multiple_of(n * 512, 512), 512)
            rows = held[a, s2, :, :, cols].reshape(256, 512)
            got = jnp.dot(chosen, rows, preferred_element_type=F32).astype(BF)
            packed[a, r, :, :, :, cols] = got.reshape(4, 2, 32, 512)

        k = third[a][r]
        far, right, left = mod4(n3 + 2), mod4(n3 + 1), mod4(n3 + 3)
        wire.go(k[0], packed.at[a, r, far, 0], relay.at[a, r, 0], dim, 1)
        wire.go(k[1], packed.at[a, r, far, 1], relay.at[a, r, 1], dim, 3)
        wire.go(k[2], packed.at[a, r, right], outs[a].at[:, n3, s2], dim, 1)
        wire.go(k[3], packed.at[a, r, left], outs[a].at[:, n3, s2], dim, 3)
        c = pltpu.make_async_copy(packed.at[a, r, n3], outs[a].at[:, n3, s2], local.at[6 + a * 4 + r])
        c.start()
        moved.append(c)

    def relays(a, r):
        n2, n1 = at[a]
        dim = ORDERS[a][2]
        n3 = place.at[dim]
        s2 = mod4(n2 + r)
        k = third[a][r]
        wire.got(k[0], relay.at[a, r, 0])
        wire.go(k[4], relay.at[a, r, 0], outs[a].at[0, mod4(n3 + 3), s2], dim, 1)
        wire.got(k[1], relay.at[a, r, 1])
        wire.go(k[5], relay.at[a, r, 1], outs[a].at[1, mod4(n3 + 1), s2], dim, 3)

    for a in range(3):
        n2, n1 = at[a]
        for i, by in enumerate((1, 2, 3)):
            wire.got(mk2[a][i], meta.at[a, mod4(n2 + 4 - by)])
    for b in (1, 2):
        for a in range(3):
            pass_on(a, ORDERS[a][1], second[a][b], *views2(a, b))
    for a in range(3):
        pack(a, 0)
    for a in range(3):
        pass_on(a, ORDERS[a][1], second[a][3], *views2(a, 3))
    for a in range(3):
        for b in range(4):
            rest(second[a][b], *views2(a, b))
    for r in (1, 3):
        for a in range(3):
            pack(a, r)
        for a in range(3):
            relays(a, 0 if r == 1 else 1)
    for a in range(3):
        n2, n1 = at[a]
        for b in range(4):
            s1 = mod4(n1 + rel1[b])
            wire.got(second[a][b][2][0], half(a, mod4(n2 + 2), s1, 0))
            wire.got(second[a][b][2][1], half(a, mod4(n2 + 2), s1, 1))
        pack(a, 2)
    for r in (3, 2):
        for a in range(3):
            relays(a, r)
    c = pltpu.make_async_copy(meta, meta_out, local.at[18])
    c.start()
    moved.append(c)
    for r in (0, 1, 3, 2):
        for a in range(3):
            n2, n1 = at[a]
            n3 = place.at[ORDERS[a][2]]
            s2 = mod4(n2 + r)
            k = third[a][r]
            wire.got(k[2], outs[a].at[:, mod4(n3 + 3), s2])
            wire.got(k[3], outs[a].at[:, mod4(n3 + 1), s2])
            wire.got(k[4], outs[a].at[0, mod4(n3 + 2), s2])
            wire.got(k[5], outs[a].at[1, mod4(n3 + 2), s2])
    for c in moved:
        c.wait()
    wire.drain()


N_DISPATCH = 3 * 6 + 12 * 6 + 18 + 72


def dispatch(tok, tan, adj, meta):
    vmem = pl.BlockSpec(memory_space=pltpu.VMEM)
    hbm = pl.BlockSpec(memory_space=pl.ANY)
    rows = jax.ShapeDtypeStruct((2, 4, 4, 32, D), BF)
    return pl.pallas_call(
        dispatch_kernel,
        out_shape=(rows, rows, rows, jax.ShapeDtypeStruct((3, 4, 4, 8, 128), F32)),
        in_specs=[vmem] * 4,
        out_specs=(hbm, hbm, hbm, hbm),
        scratch_shapes=[
            pltpu.VMEM((3, 4, 4, TOK, D), BF),
            pltpu.VMEM((3, 4, 4, 2, 32, D), BF),
            pltpu.VMEM((3, 4, 2, 32, D), BF),
            pltpu.VMEM((3, 4, 4, 8, 128), F32),
            pltpu.VMEM((256, 256), BF),
            pltpu.SemaphoreType.DMA((N_DISPATCH,)),
            pltpu.SemaphoreType.DMA((N_DISPATCH,)),
            pltpu.SemaphoreType.DMA((19,)),
        ],
        compiler_params=pltpu.CompilerParams(
            collective_id=1, has_side_effects=True, vmem_limit_bytes=56 * 2**20
        ),
        name="dispatch",
    )(tok, tan, adj, meta)


NT = (((1,), (1,)), ((), ()))


def expert_kernel(r0, r1, r2, wg, wu, wd, s0, s1, s2,
                  pre, lin, dirg, diru, back, pg, pu):
    x, v, c = (r[0].reshape(512, D) for r in (r0, r1, r2))

    @pl.loop(0, 3)
    def _(n):
        cols = pl.ds(pl.multiple_of(n * 256, 256), 256)

        def put(ref, value):
            ref[:, :, :, :, cols] = value.reshape(4, 4, 4, 8, 256)

        g, u = wg[0, :, cols], wu[0, :, cols]
        put(pre, jnp.dot(x, g, preferred_element_type=F32))
        put(dirg, jnp.dot(v, g, preferred_element_type=F32))
        put(lin, jnp.dot(x, u, preferred_element_type=F32))
        put(diru, jnp.dot(v, u, preferred_element_type=F32))
        put(back, lax.dot_general(c, wd[0, cols, :], NT, preferred_element_type=F32))

    @pl.loop(0, 16)
    def _(i):
        z, xx = i // 4, i % 4
        for y in range(4):
            p, l = pre[z, xx, y], lin[z, xx, y]
            pd, ld = dirg[y, z, xx], diru[y, z, xx]
            b = back[xx, y, z]
            s = jax.nn.sigmoid(p)
            one = s * (1.0 + p * (1.0 - s))
            two = s * (1.0 - s) * (2.0 + p * (1.0 - 2.0 * s))
            pre[z, xx, y] = b * (ld * one + l * two * pd)
            lin[z, xx, y] = b * one * pd

    for a, out in enumerate((s0, s1, s2)):
        f0, f = PARTS[a]

        @pl.loop(0, 16)
        def _(i):
            p, q = i // 4, i % 4
            at = pl.ds(pl.multiple_of(i * 32, 32), 32)
            for src, dst in ((pre, pg), (lin, pu)):
                if a == 0:
                    rows = src[p, q]
                elif a == 1:
                    rows = src[q, :, p]
                else:
                    rows = src[:, p, q]
                dst[at, :] = rows.reshape(32, FF).astype(BF)

        left, up = pg[...], pu[...]
        done = 0
        while done < f:
            n = min(256, f - done)
            got = lax.dot_general(left, wg[0, f0 + done : f0 + done + n, :], NT, preferred_element_type=F32)
            got += lax.dot_general(up, wu[0, f0 + done : f0 + done + n, :], NT, preferred_element_type=F32)
            out[:, :, 0, :, done : done + n] = got.astype(BF).reshape(4, 4, 32, n)
            done += n


def experts(r0, r1, r2, wg, wu, wd):
    rows = pl.BlockSpec((1, 4, 4, 32, D), lambda j: (j, 0, 0, 0, 0))
    wide = pl.BlockSpec((1, D, FF), lambda j: (j, 0, 0))
    tall = pl.BlockSpec((1, FF, D), lambda j: (j, 0, 0))
    return pl.pallas_call(
        expert_kernel,
        grid=(2,),
        out_shape=tuple(jax.ShapeDtypeStruct((4, 4, 2, 32, f), BF) for _, f in PARTS),
        in_specs=[rows, rows, rows, wide, wide, tall],
        out_specs=tuple(pl.BlockSpec((4, 4, 1, 32, f), lambda j: (0, 0, j, 0, 0)) for _, f in PARTS),
        scratch_shapes=[pltpu.VMEM((4, 4, 4, 8, FF), F32)] * 5 + [pltpu.VMEM((512, FF), BF)] * 2,
        compiler_params=pltpu.CompilerParams(vmem_limit_bytes=60 * 2**20),
        name="experts",
    )(r0, r1, r2, wg, wu, wd)


def collect_kernel(s0, s1, s2, meta, tan, hvp, ratio, *scratch):
    place = Place()
    n_part = 9
    parts = [scratch[i * n_part : (i + 1) * n_part] for i in range(3)]
    grown, spin, sums, send, recv, local = scratch[3 * n_part :]
    wire = Wire(place, send, recv)
    srcs = (s0, s1, s2)
    barrier(place, True)
    keys = [[wire.take() for _ in range(18)] for _ in range(3)]
    tot = [[wire.take() for _ in range(3)] for _ in range(3)]
    cross = wire.take()
    at = [tuple(place.at[d] for d in ORDERS[a]) for a in range(3)]

    moved = []
    for a in range(3):
        back, relay = parts[a][0], parts[a][1]
        n3, dim = at[a][2], ORDERS[a][2]
        k = keys[a]
        far = mod4(n3 + 2)
        wire.go(k[0], srcs[a].at[far, pl.ds(0, 2)], relay.at[0], dim, 1)
        wire.go(k[1], srcs[a].at[far, pl.ds(2, 2)], relay.at[1], dim, 3)
        wire.go(k[2], srcs[a].at[mod4(n3 + 1)], back.at[:, n3], dim, 1)
        wire.go(k[3], srcs[a].at[mod4(n3 + 3)], back.at[:, n3], dim, 3)
        c = pltpu.make_async_copy(srcs[a].at[n3], back.at[:, n3], local.at[a])
        c.start()
        moved.append(c)

    t = tan[...].astype(F32)
    sums[3, 1] = jnp.sum((t * t).reshape(8, 8, 16, 128), axis=(0, 2))

    for a in range(3):
        back, relay = parts[a][0], parts[a][1]
        n3, dim = at[a][2], ORDERS[a][2]
        k = keys[a]
        wire.got(k[0], relay.at[0])
        wire.go(k[4], relay.at[0], back.at[pl.ds(0, 2), mod4(n3 + 3)], dim, 1)
        wire.got(k[1], relay.at[1])
        wire.go(k[5], relay.at[1], back.at[pl.ds(2, 2), mod4(n3 + 1)], dim, 3)

    slots = lax.broadcasted_iota(jnp.int32, (32, 256), 0).astype(F32)
    for a in range(3):
        for r in range(4):
            s2 = mod4(at[a][1] + r)
            index, weight = column_terms(meta, a, s2, place)
            for e in range(8):
                spin[pl.ds(32 * e, 32), :] = jnp.where(index[e : e + 1, :] == slots, weight[e : e + 1, :], 0.0)
            w = spin[...].T
            high = w.astype(BF)
            grown[a, r, 0] = high
            grown[a, r, 1] = (w - high.astype(F32)).astype(BF)

    for c in moved:
        c.wait()

    def total(a, r):
        back = parts[a][0]
        s2 = mod4(at[a][1] + r)
        rows = back[s2].reshape(256, PARTS[a][1])
        got = jnp.dot(grown[a, r, 0], rows, preferred_element_type=F32)
        return got + jnp.dot(grown[a, r, 1], rows, preferred_element_type=F32)

    for a in range(3):
        back, relay, own, out2, mid2, to2, in2, *_ = parts[a]
        n1, n2, n3 = at[a]
        k, f = keys[a], PARTS[a][1]
        wire.got(k[2], back.at[:, mod4(n3 + 3)])
        wire.got(k[3], back.at[:, mod4(n3 + 1)])
        wire.got(k[4], back.at[pl.ds(0, 2), mod4(n3 + 2)])
        wire.got(k[5], back.at[pl.ds(2, 2), mod4(n3 + 2)])
        out2[...] = total(a, 2).astype(BF).reshape(4, 64, f)
        dim = ORDERS[a][1]
        wire.go(k[6], out2.at[pl.ds(0, 2)], mid2.at[0], dim, 1)
        wire.go(k[7], out2.at[pl.ds(2, 2)], mid2.at[1], dim, 3)
    for a in range(3):
        back, relay, own, out2, mid2, to2, in2, *_ = parts[a]
        own[...] = total(a, 0).reshape(4, 64, PARTS[a][1])
    for a in range(3):
        back, relay, own, out2, mid2, to2, in2, *_ = parts[a]
        k, f, dim = keys[a], PARTS[a][1], ORDERS[a][1]
        for side, r in ((0, 1), (1, 3)):
            got = total(a, r).reshape(4, 64, f)
            wire.got(k[6 + side], mid2.at[side])
            came = mid2[side].astype(F32)
            lo, hi = got[0:2], got[2:4]
            if side == 0:
                lo = lo + came
            else:
                hi = hi + came
            to2[side, 0:2] = lo.astype(BF)
            to2[side, 2:4] = hi.astype(BF)
            wire.go(k[8 + side], to2.at[side], in2.at[side], dim, r)

    for a in range(3):
        back, relay, own, out2, mid2, to2, in2, out1, mid1 = parts[a]
        n1, n2, n3 = at[a]
        k, f, dim = keys[a], PARTS[a][1], ORDERS[a][0]
        wire.got(k[8], in2.at[0])
        wire.got(k[9], in2.at[1])
        for s in range(4):
            own[s] = own[s] + (in2[0, s].astype(F32) + in2[1, s].astype(F32))
        out1[0] = own[mod4(n1 + 2)].astype(BF)
        wire.go(k[10], out1.at[0, pl.ds(0, 32)], mid1.at[0, pl.ds(0, 32)], dim, 1)
        wire.go(k[11], out1.at[0, pl.ds(32, 32)], mid1.at[0, pl.ds(32, 32)], dim, 3)
    for a in range(3):
        back, relay, own, out2, mid2, to2, in2, out1, mid1 = parts[a]
        n1, n2, n3 = at[a]
        k, f, dim = keys[a], PARTS[a][1], ORDERS[a][0]
        for side, r in ((0, 1), (1, 3)):
            rows = pl.ds(32 * side, 32)
            rest = pl.ds(32 - 32 * side, 32)
            wire.got(k[10 + side], mid1.at[0, rows])
            s = mod4(n1 + r)
            out1[1 + side, rows] = (own[s, rows] + mid1[0, rows].astype(F32)).astype(BF)
            out1[1 + side, rest] = own[s, rest].astype(BF)
            wire.go(k[12 + side], out1.at[1 + side], mid1.at[1 + side], dim, r)
    square = jnp.zeros((8, 128), F32)
    for a in range(3):
        back, relay, own, out2, mid2, to2, in2, out1, mid1 = parts[a]
        n1, n2, n3 = at[a]
        k = keys[a]
        f0, f = PARTS[a]
        wire.got(k[12], mid1.at[1])
        wire.got(k[13], mid1.at[2])
        got = own[n1] + (mid1[1].astype(F32) + mid1[2].astype(F32))
        hvp[:, f0 : f0 + f] = got
        square = square + jnp.sum((got * got).reshape(8, 8, f // 128, 128), axis=(0, 2))

    value = (square, sums[3, 1])
    for dim in range(3):
        c = place.at[dim]
        spots = 4 * dim
        grid = sums.at[pl.ds(4 + spots, 4)]
        grid[c, 0] = value[0]
        grid[c, 1] = value[1]
        for i, by in enumerate((1, 2, 3)):
            wire.go(tot[dim][i], grid.at[c], grid.at[c], dim, by)
        for i, by in enumerate((1, 2, 3)):
            wire.got(tot[dim][i], grid.at[mod4(c + 4 - by)])
        value = tuple((grid[0, q] + grid[1, q]) + (grid[2, q] + grid[3, q]) for q in range(2))
    sums[place.dp, 0] = value[0]
    sums[place.dp, 1] = value[1]
    wire.cross(cross, sums.at[place.dp], sums.at[place.dp])
    wire.got(cross, sums.at[1 - place.dp])
    top = jnp.sum(sums[0, 0] + sums[1, 0])
    low = jnp.sum(sums[0, 1] + sums[1, 1])
    ratio[...] = jnp.full((8, 128), top, F32) / jnp.full((8, 128), low, F32)
    wire.drain()


N_COLLECT = 3 * 18 + 9 + 1


def collect(s0, s1, s2, meta, tan):
    vmem = pl.BlockSpec(memory_space=pltpu.VMEM)
    scratch = []
    for _, f in PARTS:
        scratch += [
            pltpu.VMEM((4, 4, 64, f), BF),
            pltpu.VMEM((2, 2, 64, f), BF),
            pltpu.VMEM((4, 64, f), F32),
            pltpu.VMEM((4, 64, f), BF),
            pltpu.VMEM((2, 2, 64, f), BF),
            pltpu.VMEM((2, 4, 64, f), BF),
            pltpu.VMEM((2, 4, 64, f), BF),
            pltpu.VMEM((3, 64, f), BF),
            pltpu.VMEM((3, 64, f), BF),
        ]
    scratch += [
        pltpu.VMEM((3, 4, 2, 256, 256), BF),
        pltpu.VMEM((256, 256), F32),
        pltpu.VMEM((16, 2, 8, 128), F32),
        pltpu.SemaphoreType.DMA((N_COLLECT,)),
        pltpu.SemaphoreType.DMA((N_COLLECT,)),
        pltpu.SemaphoreType.DMA((3,)),
    ]
    return pl.pallas_call(
        collect_kernel,
        out_shape=(jax.ShapeDtypeStruct((TOK, D), F32), jax.ShapeDtypeStruct((8, 128), F32)),
        in_specs=[vmem] * 5,
        out_specs=(vmem, vmem),
        scratch_shapes=scratch,
        compiler_params=pltpu.CompilerParams(
            collective_id=2, has_side_effects=True, vmem_limit_bytes=48 * 2**20
        ),
        name="collect",
    )(s0, s1, s2, meta, tan)


def local(tokens, tangent, adjoint, gates, expert_ids, w_gate, w_up, w_down):
    meta = jnp.concatenate([expert_ids.astype(F32), gates], axis=0).T
    r0, r1, r2, columns = dispatch(tokens, tangent, adjoint, meta)
    s = experts(r0, r1, r2, w_gate, w_up, w_down)
    s = [p.reshape(4, 4, 64, p.shape[-1]) for p in s]
    hvp, ratio = collect(*s, columns, tangent)
    return hvp, ratio[0, 0]


def solution(mesh):
    rows = P(("dp", "expert"), None)
    weights = P("expert", None, None)
    return jax.shard_map(
        local,
        mesh=mesh,
        in_specs=(rows,) * 5 + (weights,) * 3,
        out_specs=(rows, P()),
        check_vma=False,
    )
```

profile of v0, /device:TPU:1, one launch (start us, length us, event | category | flops | bytes accessed | tf_op | source)
XLA Modules:
  0.0 206.6 jit_solution(8043504615209484644)
XLA Ops:
  0.6 0.7 convert_element_type.3
  1.3 1.4 maximum_bitcast_fusion.meta_in
  2.7 100.7 %dispatch.1 = (bf16[2,4,4,32,2048]{4,3,2,1,0:T(8,128)(2,1)}, bf16[2,4,4,32,2048]{4,3,2,1,0:T(8,128)(2,1)}, bf16[2,4,4,32,2048]{4,3,2,1,0:T(8,128)(2,1)}, f32[3,4,4,8,128]{4,3,2,1,0:T(8,128)}) custom-call(bf16[64,2048]{1,0:T(8,128)(2,1)} %tok.1, bf16[64,2048]{1,0:T(8,128)(2,1)} %tan.3, bf16[64,2048]{1,0:T(8,128)(2,1)} %adj.1, ...), custom_call_target="tpu_custom_call" | custom-call | tf_op jit(solution)/shard_map/dispatch/pallas_call | solution.py:287
  103.3 0.0 copy-start.3
  103.3 0.0 copy-start.4
  103.4 40.0 %experts.1 = (bf16[4,4,2,32,768]{4,3,2,1,0:T(8,128)(2,1)}, bf16[4,4,2,32,640]{4,3,2,1,0:T(8,128)(2,1)}, bf16[4,4,2,32,640]{4,3,2,1,0:T(8,128)(2,1)}) custom-call(bf16[2,4,4,32,2048]{4,3,2,1,0:T(8,128)(2,1)} %get-tuple-element.11.r0, bf16[2,4,4,32,2048]{4,3,2,1,0:T(8,128)(2,1)} %get-tuple-element.12.r1, bf16[2,4,4,32,2048]{4,3,2,1,0:T(8,128)(2,1)} %get-tuple-element.13.r2, ...), custom_call_target="tpu_custom_call" | custom-call | tf_op jit(solution)/shard_map/experts/pallas_call | solution.py:373
  143.3 0.0 copy-done.3
  143.3 0.0 copy-done.4
  143.3 0.0 copy-start
  143.4 1.4 copy-done
  144.8 0.0 copy-start.1
  144.8 1.3 copy-done.1
  146.1 0.0 copy-start.2
  146.1 1.3 copy-done.2
  147.4 57.9 %collect.1 = (f32[64,2048]{1,0:T(8,128)S(1)}, f32[8,128]{1,0:T(8,128)S(1)}) custom-call(bf16[4,4,64,768]{3,2,1,0:T(8,128)(2,1)S(1)} %bitcast.6, bf16[4,4,64,640]{3,2,1,0:T(8,128)(2,1)S(1)} %bitcast.7, bf16[4,4,64,640]{3,2,1,0:T(8,128)(2,1)S(1)} %bitcast.8, f32[3,4,4,8,128]{4,3,2,1,0:T(8,128)S(1)} %copy-done.4, bf16[64,2048]{1,0:T(8,128)(2,1)S(1)} %copy-done.3), custom_call_target="tpu_custom_call" | custom-call | tf_op jit(solution)/shard_map/collect/pallas_call | solution.py:560
  205.3 0.5 slice.3
  205.8 0.8 copy.11
Async XLA Ops:
  103.3 40.0 %copy-start.3 = (bf16[64,2048]{1,0:T(8,128)(2,1)S(1)}, bf16[64,2048]{1,0:T(8,128)(2,1)}, u32[]{:S(2)}) copy-start(bf16[64,2048]{1,0:T(8,128)(2,1)} %tan.3) | copy-start | bytes 786436
  103.3 40.0 %copy-start.4 = (f32[3,4,4,8,128]{4,3,2,1,0:T(8,128)S(1)}, f32[3,4,4,8,128]{4,3,2,1,0:T(8,128)}, u32[]{:S(2)}) copy-start(f32[3,4,4,8,128]{4,3,2,1,0:T(8,128)} %get-tuple-element.17.meta) | copy-start | bytes 589828
  143.3 1.4 copy-start
  144.8 1.3 copy-start.1
  146.1 1.3 copy-start.2
where the time goes:
time: 207 us
  Pallas kernels  199 us (96%)
  local copies, waits for them, and re-layouts  5.35 us (3%)
    pallas_call x1, Pallas kernels, dispatch(): pl.pallas_call(dispatch_kernel, out_shape=(rows, rows, rows, jax.ShapeDty...  101 us
    pallas_call x1, Pallas kernels, collect(): pl.pallas_call(collect_kernel, out_shape=(jax.ShapeDtypeStruct((TOK, D),...  57.9 us
    pallas_call x1, Pallas kernels, experts(): pl.pallas_call(expert_kernel, grid=(2,), out_shape=tuple((jax.ShapeDtypeS...  40 us
    unnamed x11, local copies, waits for them, and re-layouts  4.84 us

commit v1 on v0

v1 whole, which is shorter than its diff:
```python
import functools

import jax
import jax.numpy as jnp
from jax import lax
from jax.experimental import pallas as pl
from jax.experimental.pallas import tpu as pltpu
from jax.sharding import PartitionSpec as P

MESH = pl.DeviceIdType.MESH
STRIDE = (16, 4, 1)
ORDERS = ((0, 1, 2), (1, 2, 0), (2, 0, 1))
PARTS = (
    ((0, 0, 256), (1, 768, 256), (2, 1408, 256)),
    ((0, 256, 256), (1, 1024, 256), (2, 1664, 256)),
    ((0, 512, 256), (1, 1280, 128), (2, 1920, 128)),
)
TOK, D, FF, R = 64, 2048, 768, 4
BF, F32 = jnp.bfloat16, jnp.float32


class Place:
    def __init__(self):
        self.me = lax.axis_index("expert")
        self.dp = lax.axis_index("dp")
        self.at = (self.me // 16, (self.me // 4) % 4, self.me % 4)

    def shifted(self, dim, by):
        c = self.at[dim]
        return self.me + (lax.rem(c + by, 4) - c) * STRIDE[dim]


def barrier(place, core):
    sem = pltpu.get_barrier_semaphore()
    for dim in range(3):
        for by in (1, 2, 3):
            pl.semaphore_signal(
                sem, inc=1, device_id=(place.dp, place.shifted(dim, by)), device_id_type=MESH
            )
    if core:
        pl.semaphore_signal(sem, inc=1, device_id=(1 - place.dp, place.me), device_id_type=MESH)
    pl.semaphore_wait(sem, 10 if core else 9)


class Wire:
    def __init__(self, place, send, recv):
        self.place, self.send, self.recv, self.used, self.open = place, send, recv, 0, []

    def take(self):
        self.used += 1
        return self.used - 1

    def _copy(self, src, dst, k, target):
        return pltpu.make_async_remote_copy(
            src_ref=src, dst_ref=dst, send_sem=self.send.at[k], recv_sem=self.recv.at[k],
            device_id=target, device_id_type=MESH,
        )

    def go(self, k, src, dst, dim, by):
        c = self._copy(src, dst, k, (self.place.dp, self.place.shifted(dim, by)))
        c.start()
        self.open.append(c)
        return c

    def cross(self, k, src, dst):
        c = self._copy(src, dst, k, (1 - self.place.dp, self.place.me))
        c.start()
        self.open.append(c)

    def got(self, k, view):
        self._copy(view, view, k, (self.place.dp, self.place.shifted(0, 1))).wait_recv()

    def sent(self, copies):
        for c in copies:
            c.wait_send()
        self.open = [c for c in self.open if all(c is not d for d in copies)]

    def drain(self):
        self.sent(list(self.open))


def mod4(v):
    return lax.rem(v, 4)


def column_terms(meta, a, s2, place):
    dim = ORDERS[a][2]
    blocks = [meta[a, s2, s] for s in range(4)]
    low = lax.broadcasted_iota(jnp.int32, (8, 128), 1) < 64
    turn = [pltpu.roll(b, 64, 1) for b in blocks]
    ids = jnp.concatenate([jnp.where(low, blocks[0], turn[1]), jnp.where(low, blocks[2], turn[3])], axis=1)
    gates = jnp.concatenate([jnp.where(low, turn[0], blocks[1]), jnp.where(low, turn[2], blocks[3])], axis=1)
    row = lax.broadcasted_iota(jnp.int32, (8, 256), 0)
    named = jnp.zeros((8, 256), F32)
    weight = jnp.zeros((8, 256), F32)
    for r in range(8):
        e = 2 * (place.me + (r // 2 - place.at[dim]) * STRIDE[dim]) + r % 2
        hit = ids == e.astype(F32)
        n = jnp.sum(jnp.where(hit, 1.0, 0.0), axis=0, keepdims=True)
        g = jnp.sum(jnp.where(hit, gates, 0.0), axis=0, keepdims=True)
        named = jnp.where(row == r, n, named)
        weight = jnp.where(row == r, g, weight)
    i = lax.broadcasted_iota(jnp.int32, (256, 256), 0)
    l = lax.broadcasted_iota(jnp.int32, (256, 256), 1)
    upper = jnp.where((i // 64 == l // 64) & (i < l), 1.0, 0.0).astype(BF)
    before = jnp.dot(named.astype(BF), upper, preferred_element_type=F32)
    base = (lax.broadcasted_iota(jnp.int32, (8, 256), 1) // 64 * 8).astype(F32)
    return jnp.where(named > 0.5, base + before, -1.0), weight


NT = (((1,), (1,)), ((), ()))


def dispatch_kernel(tok, tan, adj, ids, gates, wg_in, wu_in, wd_in,
                    r0, r1, r2, p0, p1, grown,
                    held, packed, relay, meta, chunk, wg, wu, wd, pre, lin, dirg, diru, back,
                    table, pick, spin, grow, send, recv, local):
    place = Place()
    wire = Wire(place, send, recv)
    outs = (r0, r1, r2)
    at = [(place.at[ORDERS[a][1]], place.at[ORDERS[a][0]]) for a in range(3)]
    spots = iter(range(64))

    def copy(src, dst):
        c = pltpu.make_async_copy(src, dst, local.at[next(spots)])
        c.start()
        return c

    own = [copy(src, held.at[a, at[a][0], at[a][1]]) for a, src in enumerate((tok, tan, adj))]
    heavy = [copy(wg_in, wg), copy(wu_in, wu), copy(wd_in, wd)]
    table[...] = jnp.zeros((128, 128), F32)
    table[0:64, 0:8] = ids[...].astype(F32)
    table[64:128, 0:8] = gates[...]
    turned = table[...].T
    for a in range(3):
        meta[a, at[a][0], at[a][1]] = turned[0:8]
    barrier(place, False)
    for c in own:
        c.wait()

    def half(a, s2, s1, h):
        return held.at[a, s2, s1, pl.ds(32 * h, 32)]

    def spread(a, dim, at2, at1, keys):
        for h in (0, 1):
            wire.go(keys[0][h], half(a, at2, at1, h), half(a, at2, at1, h), dim, 1)
            wire.go(keys[1][1 - h], half(a, at2, at1, 1 - h), half(a, at2, at1, 1 - h), dim, 3)

    def keys_of():
        return ((wire.take(), wire.take()), (wire.take(), wire.take()), (wire.take(), wire.take()))

    first = [keys_of() for _ in range(3)]
    second = [[keys_of() for _ in range(4)] for _ in range(3)]
    rel1 = (0, 3, 1, 2)

    mk1 = [[wire.take() for _ in range(3)] for _ in range(3)]
    mk2 = [[wire.take() for _ in range(3)] for _ in range(3)]
    for a in range(3):
        n2, n1 = at[a]
        for i, by in enumerate((1, 2, 3)):
            wire.go(mk1[a][i], meta.at[a, n2, n1], meta.at[a, n2, n1], ORDERS[a][0], by)
    for a in range(3):
        n2, n1 = at[a]
        spread(a, ORDERS[a][0], n2, n1, first[a])
    for a in range(3):
        n2, n1 = at[a]
        spread(a, ORDERS[a][1], n2, n1, second[a][0])
    for a in range(3):
        n2, n1 = at[a]
        for i, by in enumerate((1, 2, 3)):
            wire.got(mk1[a][i], meta.at[a, n2, mod4(n1 + 4 - by)])
        for i, by in enumerate((1, 2, 3)):
            wire.go(mk2[a][i], meta.at[a, n2], meta.at[a, n2], ORDERS[a][1], by)

    def pass_on(a, dim, keys, minus, plus):
        wire.got(keys[0][0], minus(0))
        wire.go(keys[2][0], minus(0), minus(0), dim, 1)
        wire.got(keys[1][1], plus(1))
        wire.go(keys[2][1], plus(1), plus(1), dim, 3)

    def rest(keys, minus, plus):
        wire.got(keys[0][1], minus(1))
        wire.got(keys[1][0], plus(0))

    def views1(a):
        n2, n1 = at[a]
        return (lambda h: half(a, n2, mod4(n1 + 3), h)), (lambda h: half(a, n2, mod4(n1 + 1), h))

    def views2(a, b):
        n2, n1 = at[a]
        s1 = mod4(n1 + rel1[b])
        return (lambda h: half(a, mod4(n2 + 3), s1, h)), (lambda h: half(a, mod4(n2 + 1), s1, h))

    for a in range(3):
        pass_on(a, ORDERS[a][0], first[a], *views1(a))
    for a in range(3):
        rest(first[a], *views1(a))
        n2, n1 = at[a]
        for b in (1, 2):
            spread(a, ORDERS[a][1], n2, mod4(n1 + rel1[b]), second[a][b])
    for a in range(3):
        pass_on(a, ORDERS[a][1], second[a][0], *views2(a, 0))
    for a in range(3):
        n2, n1 = at[a]
        wire.got(first[a][2][0], half(a, n2, mod4(n1 + 2), 0))
        wire.got(first[a][2][1], half(a, n2, mod4(n1 + 2), 1))
        spread(a, ORDERS[a][1], n2, mod4(n1 + 2), second[a][3])

    slots = lax.broadcasted_iota(jnp.int32, (32, 256), 0).astype(F32)
    stored = []

    def weigh(a, r):
        index, weight = column_terms(meta, a, mod4(at[a][0] + r), place)
        for e in range(8):
            spin[pl.ds(32 * e, 32), :] = jnp.where(index[e : e + 1, :] == slots, weight[e : e + 1, :], 0.0)
        w = spin[...].T
        high = w.astype(BF)
        n = len(stored)
        if n >= 2:
            stored[n - 2].wait()
        grow[n % 2, 0] = high
        grow[n % 2, 1] = (w - high.astype(F32)).astype(BF)
        stored.append(copy(grow.at[n % 2], grown.at[a, r]))

    third = [[[wire.take() for _ in range(6)] for _ in range(4)] for _ in range(3)]
    going, kept = {}, {}
    turn = {0: 0, 1: 1, 3: 0, 2: 1}

    def pack(a, r):
        n2, n1 = at[a]
        dim = ORDERS[a][2]
        n3 = place.at[dim]
        s2 = mod4(n2 + r)
        buf = turn[r]
        index, _ = column_terms(meta, a, s2, place)
        for e in range(8):
            pick[pl.ds(32 * e, 32), :] = jnp.where(index[e : e + 1, :] == slots, 1.0, 0.0).astype(BF)
        chosen = pick[...]
        if r in (3, 2):
            before = 0 if r == 3 else 1
            wire.sent(going.pop((a, before)))
            kept[a, before].wait()

        @pl.loop(0, 4)
        def _(n):
            cols = pl.ds(pl.multiple_of(n * 512, 512), 512)
            rows = held[a, s2, :, :, cols].reshape(256, 512)
            got = jnp.dot(chosen, rows, preferred_element_type=F32).astype(BF)
            packed[a, buf, :, :, :, cols] = got.reshape(4, 2, 32, 512)

        k = third[a][r]
        far, right, left = mod4(n3 + 2), mod4(n3 + 1), mod4(n3 + 3)
        going[a, r] = [
            wire.go(k[0], packed.at[a, buf, far, 0], relay.at[a, r, 0], dim, 1),
            wire.go(k[1], packed.at[a, buf, far, 1], relay.at[a, r, 1], dim, 3),
            wire.go(k[2], packed.at[a, buf, right], outs[a].at[:, n3, s2], dim, 1),
            wire.go(k[3], packed.at[a, buf, left], outs[a].at[:, n3, s2], dim, 3),
        ]
        kept[a, r] = copy(packed.at[a, buf, n3], outs[a].at[:, n3, s2])

    def relays(a, r):
        n2, n1 = at[a]
        dim = ORDERS[a][2]
        n3 = place.at[dim]
        s2 = mod4(n2 + r)
        k = third[a][r]
        wire.got(k[0], relay.at[a, r, 0])
        wire.go(k[4], relay.at[a, r, 0], outs[a].at[0, mod4(n3 + 3), s2], dim, 1)
        wire.got(k[1], relay.at[a, r, 1])
        wire.go(k[5], relay.at[a, r, 1], outs[a].at[1, mod4(n3 + 1), s2], dim, 3)

    def fetch(a, r):
        n3 = place.at[ORDERS[a][2]]
        s2 = mod4(at[a][0] + r)
        k = third[a][r]
        wire.got(k[2], outs[a].at[:, mod4(n3 + 3), s2])
        wire.got(k[3], outs[a].at[:, mod4(n3 + 1), s2])
        wire.got(k[4], outs[a].at[0, mod4(n3 + 2), s2])
        wire.got(k[5], outs[a].at[1, mod4(n3 + 2), s2])
        return copy(outs[a].at[:, :, s2], chunk.at[a, turn[r]])

    def layer(a, r):
        s2 = mod4(at[a][0] + r)
        buf = turn[r]

        @pl.loop(0, 6)
        def _(i):
            j, n = i // 3, i % 3
            cols = pl.ds(pl.multiple_of(n * 256, 256), 256)
            rows = chunk[a, buf, j].reshape(128, D)
            if a == 2:
                got = lax.dot_general(rows, wd[j, cols, :], NT, preferred_element_type=F32)
                back[j, :, s2, :, :, cols] = got.reshape(4, 4, 8, 256)
            else:
                x, y = (pre, lin) if a == 0 else (dirg, diru)
                got = jnp.dot(rows, wg[j, :, cols], preferred_element_type=F32)
                x[j, :, s2, :, :, cols] = got.reshape(4, 4, 8, 256)
                got = jnp.dot(rows, wu[j, :, cols], preferred_element_type=F32)
                y[j, :, s2, :, :, cols] = got.reshape(4, 4, 8, 256)

    def layers(r):
        for a in range(3):
            if r in (3, 2):
                kept[a, r].wait()
        loads = [fetch(a, r) for a in range(3)]
        for a in range(3):
            loads[a].wait()
            layer(a, r)

    for a in range(3):
        n2, n1 = at[a]
        for i, by in enumerate((1, 2, 3)):
            wire.got(mk2[a][i], meta.at[a, mod4(n2 + 4 - by)])
    for a in range(3):
        pack(a, 0)
    for b in (1, 2):
        for a in range(3):
            pass_on(a, ORDERS[a][1], second[a][b], *views2(a, b))
            weigh(a, 2 * b - 2)
            weigh(a, 2 * b - 1)
    for a in range(3):
        pass_on(a, ORDERS[a][1], second[a][3], *views2(a, 3))
    for a in range(3):
        for b in range(4):
            rest(second[a][b], *views2(a, b))
        pack(a, 1)
    for a in range(3):
        relays(a, 0)
    for a in range(3):
        n2, n1 = at[a]
        for b in range(4):
            s1 = mod4(n1 + rel1[b])
            wire.got(second[a][b][2][0], half(a, mod4(n2 + 2), s1, 0))
            wire.got(second[a][b][2][1], half(a, mod4(n2 + 2), s1, 1))
    for a in range(3):
        pack(a, 3)
    for a in range(3):
        relays(a, 1)
    for c in heavy:
        c.wait()
    layers(0)
    for a in range(3):
        pack(a, 2)
    for a in range(3):
        relays(a, 3)
    layers(1)
    for a in range(3):
        relays(a, 2)
    layers(3)
    layers(2)
    wire.drain()

    written = []
    for j in range(2):

        @pl.loop(0, 24)
        def _(i):
            n, q = i % 3, i // 3
            zp, xp, yp = q // 4, (q // 2) % 2, q % 2
            cols = pl.ds(pl.multiple_of(n * 256, 256), 256)
            cols_up = pl.ds(pl.multiple_of(FF + n * 256, 256), 256)
            part = {}
            for dz in range(2):
                for dx in range(2):
                    for dy in range(2):
                        z, x, y = 2 * zp + dz, 2 * xp + dx, 2 * yp + dy
                        p, l = pre[j, z, x, y, :, cols], lin[j, z, x, y, :, cols]
                        pd, ld = dirg[j, y, z, x, :, cols], diru[j, y, z, x, :, cols]
                        b = back[j, x, y, z, :, cols]
                        s = jax.nn.sigmoid(p)
                        one = s * (1.0 + p * (1.0 - s))
                        two = s * (1.0 - s) * (2.0 + p * (1.0 - 2.0 * s))
                        part[dz, dx, dy] = (b * (ld * one + l * two * pd), b * one * pd)

            def put(a, hi, lo, d_hi, d_lo, inner, pair):
                rows = pl.ds(pl.multiple_of(16 * inner, 16), 16)
                for which, where in ((0, cols), (1, cols_up)):
                    value = jnp.concatenate([v[which] for v in pair], axis=0).astype(BF)
                    if j == 0:
                        chunk[a, hi, d_hi, 2 * lo + d_lo, rows, where] = value
                    else:
                        packed[a, hi, 2 * d_hi + lo, d_lo, rows, where] = value

            for u in range(2):
                for w in range(2):
                    put(0, zp, xp, u, w, yp, (part[u, w, 0], part[u, w, 1]))
                    put(1, yp, zp, u, w, xp, (part[w, 0, u], part[w, 1, u]))
                    put(2, xp, yp, u, w, zp, (part[0, u, w], part[1, u, w]))

        for a in range(3):
            src, dst = (chunk, p0) if j == 0 else (packed, p1)
            written.append(copy(src.at[a, :, :, :, :, pl.ds(0, 2 * FF)], dst.at[a]))
    for c in written:
        c.wait()
    for c in stored[-2:]:
        c.wait()


N_DISPATCH = 3 * 6 + 12 * 6 + 18 + 72


def dispatch(tok, tan, adj, ids, gates, wg, wu, wd):
    vmem = pl.BlockSpec(memory_space=pltpu.VMEM)
    hbm = pl.BlockSpec(memory_space=pl.ANY)
    rows = jax.ShapeDtypeStruct((2, 4, 4, 32, D), BF)
    out = pl.pallas_call(
        dispatch_kernel,
        out_shape=(
            rows, rows, rows,
            jax.ShapeDtypeStruct((3, 2, 2, 4, 32, 2 * FF), BF),
            jax.ShapeDtypeStruct((3, 2, 4, 2, 32, 2 * FF), BF),
            jax.ShapeDtypeStruct((3, 4, 2, 256, 256), BF),
        ),
        in_specs=[hbm] * 3 + [vmem] * 2 + [hbm] * 3,
        out_specs=(hbm,) * 6,
        scratch_shapes=[
            pltpu.VMEM((3, 4, 4, TOK, D), BF),
            pltpu.VMEM((3, 2, 4, 2, 32, D), BF),
            pltpu.VMEM((3, 4, 2, 32, D), BF),
            pltpu.VMEM((3, 4, 4, 8, 128), F32),
            pltpu.VMEM((3, 2, 2, 4, 32, D), BF),
            pltpu.VMEM((2, D, FF), BF),
            pltpu.VMEM((2, D, FF), BF),
            pltpu.VMEM((2, FF, D), BF),
        ]
        + [pltpu.VMEM((2, 4, 4, 4, 8, FF), F32)] * 5
        + [
            pltpu.VMEM((128, 128), F32),
            pltpu.VMEM((256, 256), BF),
            pltpu.VMEM((256, 256), F32),
            pltpu.VMEM((2, 2, 256, 256), BF),
            pltpu.SemaphoreType.DMA((N_DISPATCH,)),
            pltpu.SemaphoreType.DMA((N_DISPATCH,)),
            pltpu.SemaphoreType.DMA((64,)),
        ],
        compiler_params=pltpu.CompilerParams(
            collective_id=1, has_side_effects=True, vmem_limit_bytes=67043328
        ),
        name="dispatch",
    )(tok, tan, adj, ids, gates, wg, wu, wd)
    return out[3:]


def collect_kernel(p0, p1, wg_in, wu_in, grown_in, tan, hvp, ratio, *scratch):
    place = Place()
    n_part = 10
    parts = [scratch[i * n_part : (i + 1) * n_part] for i in range(9)]
    left, wg, wu, grown, sums, send, recv, local = scratch[9 * n_part :]
    wire = Wire(place, send, recv)
    spots = iter(range(64))

    def copy(src, dst):
        c = pltpu.make_async_copy(src, dst, local.at[next(spots)])
        c.start()
        return c

    loads = {}
    for q in range(3):
        for a, f0, n in PARTS[q]:
            got = []
            if q == 0:
                got = [copy(p0.at[a], left.at[0, a]), copy(p1.at[a], left.at[1, a])]
            rows = pl.ds(f0, n)
            got.append(copy(wg_in.at[:, rows], wg.at[:, rows]))
            got.append(copy(wu_in.at[:, rows], wu.at[:, rows]))
            loads[q, a] = got
        if q == 0:
            grown_load = copy(grown_in, grown)
    barrier(place, True)
    keys = [[[wire.take() for _ in range(14)] for _ in range(3)] for _ in range(3)]
    tot = [[wire.take() for _ in range(3)] for _ in range(3)]
    cross = wire.take()
    at = [tuple(place.at[d] for d in ORDERS[a]) for a in range(3)]
    moved = {}
    state = {"square": jnp.zeros((8, 128), F32)}

    def begin(q):
        for a, f0, n in PARTS[q]:
            out, back, relay = parts[3 * q + a][:3]
            for c in loads[q, a]:
                c.wait()
            for j in range(2):
                got = lax.dot_general(left[j, a, :, 0:FF], wg[j, f0 : f0 + n, :], NT, preferred_element_type=F32)
                got += lax.dot_general(left[j, a, :, FF : 2 * FF], wu[j, f0 : f0 + n, :], NT, preferred_element_type=F32)
                out[:, :, 32 * j : 32 * j + 32, :] = got.astype(BF).reshape(4, 4, 32, n)
            n3, dim = at[a][2], ORDERS[a][2]
            k = keys[q][a]
            far = mod4(n3 + 2)
            wire.go(k[0], out.at[far, pl.ds(0, 2)], relay.at[0], dim, 1)
            wire.go(k[1], out.at[far, pl.ds(2, 2)], relay.at[1], dim, 3)
            wire.go(k[2], out.at[mod4(n3 + 1)], back.at[:, n3], dim, 1)
            wire.go(k[3], out.at[mod4(n3 + 3)], back.at[:, n3], dim, 3)
            moved[q, a] = copy(out.at[n3], back.at[:, n3])

    def relays(q):
        for a, _, _ in PARTS[q]:
            back, relay = parts[3 * q + a][1:3]
            n3, dim = at[a][2], ORDERS[a][2]
            k = keys[q][a]
            wire.got(k[0], relay.at[0])
            wire.go(k[4], relay.at[0], back.at[pl.ds(0, 2), mod4(n3 + 3)], dim, 1)
            wire.got(k[1], relay.at[1])
            wire.go(k[5], relay.at[1], back.at[pl.ds(2, 2), mod4(n3 + 1)], dim, 3)

    def total(q, a, r):
        n = PARTS[q][a][2]
        rows = parts[3 * q + a][1][mod4(at[a][1] + r)].reshape(256, n)
        got = jnp.dot(grown[a, r, 0], rows, preferred_element_type=F32)
        got = got + jnp.dot(grown[a, r, 1], rows, preferred_element_type=F32)
        return got.reshape(4, 64, n)

    def far2(q):
        for a, _, n in PARTS[q]:
            back, relay, own, out2, mid2 = parts[3 * q + a][1:6]
            n3, dim = at[a][2], ORDERS[a][1]
            k = keys[q][a]
            moved[q, a].wait()
            wire.got(k[2], back.at[:, mod4(n3 + 3)])
            wire.got(k[3], back.at[:, mod4(n3 + 1)])
            wire.got(k[4], back.at[pl.ds(0, 2), mod4(n3 + 2)])
            wire.got(k[5], back.at[pl.ds(2, 2), mod4(n3 + 2)])
            out2[...] = total(q, a, 2).astype(BF)
            wire.go(k[6], out2.at[pl.ds(0, 2)], mid2.at[0], dim, 1)
            wire.go(k[7], out2.at[pl.ds(2, 2)], mid2.at[1], dim, 3)
        for a, _, n in PARTS[q]:
            parts[3 * q + a][3][...] = total(q, a, 0)

    def near2(q):
        for a, _, n in PARTS[q]:
            mid2, to2, in2 = parts[3 * q + a][5:8]
            k, dim = keys[q][a], ORDERS[a][1]
            for side, r in ((0, 1), (1, 3)):
                got = total(q, a, r)
                wire.got(k[6 + side], mid2.at[side])
                came = mid2[side].astype(F32)
                lo, hi = got[0:2], got[2:4]
                if side == 0:
                    lo = lo + came
                else:
                    hi = hi + came
                to2[side, 0:2] = lo.astype(BF)
                to2[side, 2:4] = hi.astype(BF)
                wire.go(k[8 + side], to2.at[side], in2.at[side], dim, r)

    def far1(q):
        for a, _, n in PARTS[q]:
            own, in2, out1, mid1 = (parts[3 * q + a][i] for i in (3, 7, 8, 9))
            n1, dim = at[a][0], ORDERS[a][0]
            k = keys[q][a]
            wire.got(k[8], in2.at[0])
            wire.got(k[9], in2.at[1])
            own[...] = own[...] + (in2[0].astype(F32) + in2[1].astype(F32))
            out1[0] = own[mod4(n1 + 2)].astype(BF)
            wire.go(k[10], out1.at[0, pl.ds(0, 32)], mid1.at[0, pl.ds(0, 32)], dim, 1)
            wire.go(k[11], out1.at[0, pl.ds(32, 32)], mid1.at[0, pl.ds(32, 32)], dim, 3)

    def near1(q):
        for a, _, n in PARTS[q]:
            own, in2, out1, mid1 = (parts[3 * q + a][i] for i in (3, 7, 8, 9))
            n1, dim = at[a][0], ORDERS[a][0]
            k = keys[q][a]
            for side, r in ((0, 1), (1, 3)):
                rows = pl.ds(32 * side, 32)
                rest = pl.ds(32 - 32 * side, 32)
                wire.got(k[10 + side], mid1.at[0, rows])
                s = mod4(n1 + r)
                out1[1 + side, rows] = (own[s, rows] + mid1[0, rows].astype(F32)).astype(BF)
                out1[1 + side, rest] = own[s, rest].astype(BF)
                wire.go(k[12 + side], out1.at[1 + side], mid1.at[1 + side], dim, r)

    def finish(q):
        for a, f0, n in PARTS[q]:
            own, mid1 = parts[3 * q + a][3], parts[3 * q + a][9]
            k = keys[q][a]
            wire.got(k[12], mid1.at[1])
            wire.got(k[13], mid1.at[2])
            got = own[at[a][0]] + (mid1[1].astype(F32) + mid1[2].astype(F32))
            hvp[:, f0 : f0 + n] = got
            state["square"] += jnp.sum((got * got).reshape(8, 8, n // 128, 128), axis=(0, 2))

    begin(0)
    begin(1)
    relays(0)
    begin(2)
    relays(1)
    grown_load.wait()
    far2(0)
    relays(2)
    near2(0)
    far2(1)
    far1(0)
    near2(1)
    far2(2)
    near1(0)
    far1(1)
    near2(2)
    t = tan[...].astype(F32)
    low = jnp.sum((t * t).reshape(8, 8, 16, 128), axis=(0, 2))
    finish(0)
    near1(1)
    far1(2)
    finish(1)
    near1(2)
    finish(2)

    value = (state["square"], low)
    for dim in range(3):
        c = place.at[dim]
        grid = sums.at[pl.ds(4 + 4 * dim, 4)]
        grid[c, 0] = value[0]
        grid[c, 1] = value[1]
        for i, by in enumerate((1, 2, 3)):
            wire.go(tot[dim][i], grid.at[c], grid.at[c], dim, by)
        for i, by in enumerate((1, 2, 3)):
            wire.got(tot[dim][i], grid.at[mod4(c + 4 - by)])
        value = tuple((grid[0, q] + grid[1, q]) + (grid[2, q] + grid[3, q]) for q in range(2))
    sums[place.dp, 0] = value[0]
    sums[place.dp, 1] = value[1]
    wire.cross(cross, sums.at[place.dp], sums.at[place.dp])
    wire.got(cross, sums.at[1 - place.dp])
    top = jnp.sum(sums[0, 0] + sums[1, 0])
    low = jnp.sum(sums[0, 1] + sums[1, 1])
    ratio[...] = jnp.full((8, 128), top, F32) / jnp.full((8, 128), low, F32)
    wire.drain()


N_COLLECT = 9 * 14 + 9 + 1


def collect(p0, p1, wg, wu, grown, tan):
    vmem = pl.BlockSpec(memory_space=pltpu.VMEM)
    hbm = pl.BlockSpec(memory_space=pl.ANY)
    scratch = []
    for q in range(3):
        for _, _, f in PARTS[q]:
            scratch += [
                pltpu.VMEM((4, 4, 64, f), BF),
                pltpu.VMEM((4, 4, 64, f), BF),
                pltpu.VMEM((2, 2, 64, f), BF),
                pltpu.VMEM((4, 64, f), F32),
                pltpu.VMEM((4, 64, f), BF),
                pltpu.VMEM((2, 2, 64, f), BF),
                pltpu.VMEM((2, 4, 64, f), BF),
                pltpu.VMEM((2, 4, 64, f), BF),
                pltpu.VMEM((3, 64, f), BF),
                pltpu.VMEM((3, 64, f), BF),
            ]
    scratch += [
        pltpu.VMEM((2, 3, 512, 2 * FF), BF),
        pltpu.VMEM((2, D, FF), BF),
        pltpu.VMEM((2, D, FF), BF),
        pltpu.VMEM((3, 4, 2, 256, 256), BF),
        pltpu.VMEM((16, 2, 8, 128), F32),
        pltpu.SemaphoreType.DMA((N_COLLECT,)),
        pltpu.SemaphoreType.DMA((N_COLLECT,)),
        pltpu.SemaphoreType.DMA((64,)),
    ]
    return pl.pallas_call(
        collect_kernel,
        out_shape=(jax.ShapeDtypeStruct((TOK, D), F32), jax.ShapeDtypeStruct((8, 128), F32)),
        in_specs=[hbm] * 5 + [vmem],
        out_specs=(vmem, vmem),
        scratch_shapes=scratch,
        compiler_params=pltpu.CompilerParams(
            collective_id=2, has_side_effects=True, vmem_limit_bytes=60 * 2**20
        ),
        name="collect",
    )(p0, p1, wg, wu, grown, tan)


def local(tokens, tangent, adjoint, gates, expert_ids, w_gate, w_up, w_down):
    p0, p1, grown = dispatch(tokens, tangent, adjoint, expert_ids, gates, w_gate, w_up, w_down)
    p0, p1 = p0.reshape(3, 512, 2 * FF), p1.reshape(3, 512, 2 * FF)
    hvp, ratio = collect(p0, p1, w_gate, w_up, grown, tangent)
    return hvp, ratio[0, 0]


def solution(mesh):
    rows = P(("dp", "expert"), None)
    weights = P("expert", None, None)
    return jax.shard_map(
        local,
        mesh=mesh,
        in_specs=(rows,) * 5 + (weights,) * 3,
        out_specs=(rows, P()),
        check_vma=False,
    )
```

time: 207 us -> 200 us (0.966)
  Pallas kernels: 199 us -> 194 us
    pallas_call x1 -> x0, Pallas kernels: 40 us -> none  [experts(): pl.pallas_call(expert_kernel, grid=(2,), out_shape=tuple((jax.ShapeDtypeS...]
    pallas_call x1, Pallas kernels: 101 us -> 126 us  [dispatch(): pl.pallas_call(dispatch_kernel, out_shape=(rows, rows, rows, jax.ShapeDty...]
    pallas_call x1, Pallas kernels: 57.9 us -> 68 us  [collect(): pl.pallas_call(collect_kernel, out_shape=(jax.ShapeDtypeStruct((TOK, D),...]
    unnamed x11 -> x3, local copies, waits for them, and re-layouts: 4.84 us -> 4.65 us
where the time goes in v1:
time: 200 us
  Pallas kernels  194 us (97%)
  local copies, waits for them, and re-layouts  5.83 us (3%)
    pallas_call x1, Pallas kernels, dispatch(): pl.pallas_call(dispatch_kernel, out_shape=(rows, rows, rows, jax.ShapeDty...  126 us
    pallas_call x1, Pallas kernels, collect(): pl.pallas_call(collect_kernel, out_shape=(jax.ShapeDtypeStruct((TOK, D),...  68 us
    unnamed x3, local copies, waits for them, and re-layouts  4.65 us

profile of v1, /device:TPU:1, one launch (start us, length us, event | category | flops | bytes accessed | tf_op | source)
XLA Modules:
  0.0 200.0 jit_solution(1829873091993887359)
XLA Ops:
  0.6 1.4 copy.11.gates
  2.0 1.4 copy.10.ids
  3.4 125.5 %dispatch.1 = (bf16[2,4,4,32,2048]{4,3,2,1,0:T(8,128)(2,1)}, bf16[2,4,4,32,2048]{4,3,2,1,0:T(8,128)(2,1)}, bf16[2,4,4,32,2048]{4,3,2,1,0:T(8,128)(2,1)}, bf16[3,...) custom-call(bf16[64,2048]{1,0:T(8,128)(2,1)} %tok.1, ...), custom_call_target="tpu_custom_call" | custom-call | tf_op jit(solution)/shard_map/dispatch/pallas_call | solution.py:406
  128.9 68.0 %collect.1 = (f32[64,2048]{1,0:T(8,128)}, f32[8,128]{1,0:T(8,128)}) custom-call(bf16[3,512,1536]{2,1,0:T(8,128)(2,1)} %bitcast.3, bf16[3,512,1536]{2,1,0:T(8,128)(2,1)} %bitcast.4, bf16[2,2048,768]{2,1,0:T(8,128)(2,1)} %wg_in.3, bf16[2,2048,768]{2,1,0:T(8,128)(2,1)} %wu_in.3, bf16[3,4,2,256,256]{4,3,2,1,0:T(8,128)(2,1)} %get-tuple-element.9.grown_in, ...), custom_call_target="tpu_custom_call" | custom-call | tf_op jit(solution)/shard_map/collect/pallas_call | solution.py:658
  197.0 1.2 slice.3
  198.1 1.9 copy.13

commit v2 on v1

v2 whole, which is shorter than its diff:
```python
import functools

import jax
import jax.numpy as jnp
from jax import lax
from jax.experimental import pallas as pl
from jax.experimental.pallas import tpu as pltpu
from jax.sharding import PartitionSpec as P

MESH = pl.DeviceIdType.MESH
STRIDE = (16, 4, 1)
ORDERS = ((0, 1, 2), (1, 2, 0), (2, 0, 1))
PARTS = (
    ((0, 0, 256), (1, 768, 256), (2, 1408, 256)),
    ((0, 256, 256), (1, 1024, 256), (2, 1664, 256)),
    ((0, 512, 256), (1, 1280, 128), (2, 1920, 128)),
)
TOK, D, FF, R = 64, 2048, 768, 4
BF, F32 = jnp.bfloat16, jnp.float32


class Place:
    def __init__(self):
        self.me = lax.axis_index("expert")
        self.dp = lax.axis_index("dp")
        self.at = (self.me // 16, (self.me // 4) % 4, self.me % 4)

    def shifted(self, dim, by):
        c = self.at[dim]
        return self.me + (lax.rem(c + by, 4) - c) * STRIDE[dim]


def barrier(place):
    sem = pltpu.get_barrier_semaphore()
    for dim in range(3):
        for by in (1, 2, 3):
            pl.semaphore_signal(
                sem, inc=1, device_id=(place.dp, place.shifted(dim, by)), device_id_type=MESH
            )
    pl.semaphore_wait(sem, 9)


class Wire:
    def __init__(self, place, send, recv):
        self.place, self.send, self.recv, self.groups, self.taken = place, send, recv, 0, 0

    def group(self):
        self.groups += 1
        return self.groups - 1

    def take(self):
        self.taken += 1
        return self.taken - 1

    def _copy(self, sent, came, src, dst, target):
        return pltpu.make_async_remote_copy(
            src_ref=src, dst_ref=dst, send_sem=self.send.at[sent], recv_sem=self.recv.at[came],
            device_id=target, device_id_type=MESH,
        )

    def push(self, sent, came, src, dst, target):
        self._copy(sent, came, src, dst, target).start()

    def go(self, sent, came, src, dst, dim, by):
        self.push(sent, came, src, dst, (self.place.dp, self.place.shifted(dim, by)))

    def got(self, came, view):
        self._copy(0, came, view, view, (self.place.dp, self.place.shifted(0, 1))).wait_recv()

    def sent(self, group, view):
        self._copy(group, 0, view, view, (self.place.dp, self.place.shifted(0, 1))).wait_send()


def mod4(v):
    return lax.rem(v, 4)


def column_terms(meta, a, s2, place):
    dim = ORDERS[a][2]
    blocks = [meta[a, s2, s] for s in range(4)]
    low = lax.broadcasted_iota(jnp.int32, (8, 128), 1) < 64
    turn = [pltpu.roll(b, 64, 1) for b in blocks]
    ids = jnp.concatenate([jnp.where(low, blocks[0], turn[1]), jnp.where(low, blocks[2], turn[3])], axis=1)
    gates = jnp.concatenate([jnp.where(low, turn[0], blocks[1]), jnp.where(low, turn[2], blocks[3])], axis=1)
    row = lax.broadcasted_iota(jnp.int32, (8, 256), 0)
    named = jnp.zeros((8, 256), F32)
    weight = jnp.zeros((8, 256), F32)
    for r in range(8):
        e = 2 * (place.me + (r // 2 - place.at[dim]) * STRIDE[dim]) + r % 2
        hit = ids == e.astype(F32)
        n = jnp.sum(jnp.where(hit, 1.0, 0.0), axis=0, keepdims=True)
        g = jnp.sum(jnp.where(hit, gates, 0.0), axis=0, keepdims=True)
        named = jnp.where(row == r, n, named)
        weight = jnp.where(row == r, g, weight)
    i = lax.broadcasted_iota(jnp.int32, (256, 256), 0)
    l = lax.broadcasted_iota(jnp.int32, (256, 256), 1)
    upper = jnp.where((i // 64 == l // 64) & (i < l), 1.0, 0.0).astype(BF)
    before = jnp.dot(named.astype(BF), upper, preferred_element_type=F32)
    base = (lax.broadcasted_iota(jnp.int32, (8, 256), 1) // 64 * 8).astype(F32)
    return jnp.where(named > 0.5, base + before, -1.0), weight


NT = (((1,), (1,)), ((), ()))


def dispatch_kernel(tok, tan, adj, ids, gates, wg_in, wu_in, wd_in,
                    r0, r1, r2, b0, b1, b2, grown,
                    held, packed, relay, meta, chunk, wg, wu, wd, pre, lin, dirg, diru, back, parts,
                    o0, o1, o2, q0, q1, q2, picks, spin, grow, send, recv, local):
    place = Place()
    wire = Wire(place, send, recv)
    outs, backs, replies, passing = (r0, r1, r2), (b0, b1, b2), (o0, o1, o2), (q0, q1, q2)
    at = [(place.at[ORDERS[a][1]], place.at[ORDERS[a][0]]) for a in range(3)]

    def copy(src, dst, spot):
        c = pltpu.make_async_copy(src, dst, local.at[spot])
        c.start()
        return c

    own = [copy(src, held.at[a, at[a][0], at[a][1]], a) for a, src in enumerate((tok, tan, adj))]
    heavy = [copy(wg_in, wg, 3), copy(wu_in, wu, 4), copy(wd_in, wd, 5)]
    turned = jnp.concatenate([ids[...].astype(F32), gates[...]], axis=1)
    for a in range(3):
        meta[a, at[a][0], at[a][1]] = turned
    barrier(place)
    for c in own:
        c.wait()

    def half(a, s2, s1, h):
        return held.at[a, s2, s1, pl.ds(32 * h, 32)]

    def spread(a, dim, at2, at1, keys):
        plus, minus, rest, _, sent = keys
        wire.go(sent, plus, half(a, at2, at1, 0), half(a, at2, at1, 0), dim, 1)
        wire.go(sent, minus, half(a, at2, at1, 1), half(a, at2, at1, 1), dim, 3)
        wire.go(sent, rest, half(a, at2, at1, 1), half(a, at2, at1, 1), dim, 1)
        wire.go(sent, rest, half(a, at2, at1, 0), half(a, at2, at1, 0), dim, 3)

    first, second = [], []
    for a in range(3):
        sent = wire.group()
        first.append((wire.take(), wire.take(), wire.take(), wire.take(), sent))
        sent, rest_key, far_key = wire.group(), wire.take(), wire.take()
        second.append([(wire.take(), wire.take(), rest_key, far_key, sent) for _ in range(4)])
    rel1 = (0, 3, 1, 2)

    mk1 = [(wire.group(), wire.take()) for _ in range(3)]
    mk2 = [(wire.group(), wire.take()) for _ in range(3)]
    for a in range(3):
        n2, n1 = at[a]
        for by in (1, 2, 3):
            wire.go(*mk1[a], meta.at[a, n2, n1], meta.at[a, n2, n1], ORDERS[a][0], by)
    for a in range(3):
        n2, n1 = at[a]
        spread(a, ORDERS[a][0], n2, n1, first[a])
    for a in range(3):
        n2, n1 = at[a]
        spread(a, ORDERS[a][1], n2, n1, second[a][0])
    for a in range(3):
        n2, n1 = at[a]
        wire.got(mk1[a][1], meta.at[a, n2, pl.ds(0, 3)])
        for by in (1, 2, 3):
            wire.go(*mk2[a], meta.at[a, n2], meta.at[a, n2], ORDERS[a][1], by)

    def pass_on(a, dim, keys, minus, plus):
        from_minus, from_plus, _, far, sent = keys
        wire.got(from_minus, minus(0))
        wire.go(sent, far, minus(0), minus(0), dim, 1)
        wire.got(from_plus, plus(1))
        wire.go(sent, far, plus(1), plus(1), dim, 3)

    def views1(a):
        n2, n1 = at[a]
        return (lambda h: half(a, n2, mod4(n1 + 3), h)), (lambda h: half(a, n2, mod4(n1 + 1), h))

    def views2(a, b):
        n2, n1 = at[a]
        s1 = mod4(n1 + rel1[b])
        return (lambda h: half(a, mod4(n2 + 3), s1, h)), (lambda h: half(a, mod4(n2 + 1), s1, h))

    for a in range(3):
        pass_on(a, ORDERS[a][0], first[a], *views1(a))
    for a in range(3):
        n2, n1 = at[a]
        wire.got(first[a][2], held.at[a, n2, mod4(n1 + 1)])
        for b in (1, 2):
            spread(a, ORDERS[a][1], n2, mod4(n1 + rel1[b]), second[a][b])
    for a in range(3):
        pass_on(a, ORDERS[a][1], second[a][0], *views2(a, 0))
    for a in range(3):
        n2, n1 = at[a]
        wire.got(first[a][3], held.at[a, n2, mod4(n1 + 2)])
        spread(a, ORDERS[a][1], n2, mod4(n1 + 2), second[a][3])

    slots = lax.broadcasted_iota(jnp.int32, (32, 256), 0).astype(F32)
    stored = []

    def weigh(a, r):
        index, weight = column_terms(meta, a, mod4(at[a][0] + r), place)
        for e in range(8):
            spin[pl.ds(32 * e, 32), :] = jnp.where(index[e : e + 1, :] == slots, weight[e : e + 1, :], 0.0)
        w = spin[...].T
        high = w.astype(BF)
        for e in range(8):
            hit = jnp.where(index[e : e + 1, :] == slots, 1.0, 0.0)
            picks[a, r, e % 2, pl.ds(32 * (e // 2), 32), :] = hit.astype(BF)
        n = len(stored)
        if n >= 2:
            stored[n - 2].wait()
        grow[n % 2, 0] = high
        grow[n % 2, 1] = (w - high.astype(F32)).astype(BF)
        stored.append(copy(grow.at[n % 2], grown.at[a, r], 6 + n % 2))

    third = [[(wire.group(), wire.take(), wire.take()) for _ in range(8)] for _ in range(3)]
    fourth = [[(wire.group(), wire.take(), wire.take()) for _ in range(2)] for _ in range(3)]
    passed = [wire.group() for _ in range(3)]
    repassed = [wire.group() for _ in range(3)]
    kept = {}
    rels = (0, 1, 3, 2)

    def where(a, s):
        dim = ORDERS[a][2]
        return s // 4, place.at[dim], mod4(at[a][0] + rels[s % 4]), dim

    def settle(a, s):
        c = kept.pop((a, s), None)
        if c is not None:
            c.wait()

    def pack(s):
        for a in range(3):
            j, n3, s2, dim = where(a, s)
            buf = s % 3
            chosen = picks[a, rels[s % 4], j]
            if s >= 3:
                wire.sent(third[a][s - 3][0], packed.at[a, buf, pl.ds(0, 3)])
                settle(a, s - 3)

            @pl.loop(0, 4)
            def _(n):
                cols = pl.ds(pl.multiple_of(n * 512, 512), 512)
                rows = held[a, s2, :, :, cols].reshape(256, 512)
                got = jnp.dot(chosen, rows, preferred_element_type=F32).astype(BF)
                packed[a, buf, :, :, cols] = got.reshape(4, 32, 512)

            sent, early, _ = third[a][s]
            far = mod4(n3 + 2)
            wire.go(sent, early, packed.at[a, buf, far, pl.ds(0, 16)], relay.at[a, s, 0], dim, 1)
            wire.go(sent, early, packed.at[a, buf, far, pl.ds(16, 16)], relay.at[a, s, 1], dim, 3)

    def direct(s):
        for a in range(3):
            j, n3, s2, dim = where(a, s)
            buf = s % 3
            sent, _, late = third[a][s]
            wire.go(sent, late, packed.at[a, buf, mod4(n3 + 1)], outs[a].at[j, n3, s2], dim, 1)
            wire.go(sent, late, packed.at[a, buf, mod4(n3 + 3)], outs[a].at[j, n3, s2], dim, 3)
            kept[a, s] = copy(packed.at[a, buf, n3], outs[a].at[j, n3, s2], 8 + 3 * a + buf)

    def relays(s):
        for a in range(3):
            j, n3, s2, dim = where(a, s)
            _, early, late = third[a][s]
            sent = passed[a]
            wire.got(early, relay.at[a, s])
            wire.go(sent, late, relay.at[a, s, 0], outs[a].at[j, mod4(n3 + 3), s2, pl.ds(0, 16)], dim, 1)
            wire.go(sent, late, relay.at[a, s, 1], outs[a].at[j, mod4(n3 + 1), s2, pl.ds(16, 16)], dim, 3)

    loads = {}

    def fetch(s):
        for a in range(3):
            j, n3, s2, dim = where(a, s)
            wire.got(third[a][s][2], outs[a].at[j, pl.ds(0, 3), s2])
            settle(a, s)
            loads[a, s] = copy(outs[a].at[j, :, s2], chunk.at[a, s % 4], 17 + 4 * a + s % 4)

    def layer(s, stages):
        j, half2 = s // 4, s % 4
        for a in range(3):
            if 0 in stages:
                loads[a, s].wait()
                loads[a, s + 1].wait()
            spots2 = [where(a, s + i)[2] for i in range(2)]

            @pl.loop(min(stages), max(stages) + 1)
            def _(n):
                cols = pl.ds(pl.multiple_of(n * 256, 256), 256)
                rows = chunk[a, half2 : half2 + 2].reshape(256, D)

                def put(ref, value):
                    value = value.reshape(2, 4, 4, 8, 256)
                    for i in range(2):
                        ref[:, spots2[i], :, :, cols] = value[i]

                if a == 2:
                    put(back, lax.dot_general(rows, wd[j, cols, :], NT, preferred_element_type=F32))
                else:
                    x, y = (pre, lin) if a == 0 else (dirg, diru)
                    put(x, jnp.dot(rows, wg[j, :, cols], preferred_element_type=F32))
                    put(y, jnp.dot(rows, wu[j, :, cols], preferred_element_type=F32))

    def mix():
        @pl.loop(0, 24)
        def _(i):
            n, q = i % 3, i // 3
            zp, xp, yp = q // 4, (q // 2) % 2, q % 2
            cols = pl.ds(pl.multiple_of(n * 256, 256), 256)
            part = {}
            for dz in range(2):
                for dx in range(2):
                    for dy in range(2):
                        z, x, y = 2 * zp + dz, 2 * xp + dx, 2 * yp + dy
                        p, l = pre[z, x, y, :, cols], lin[z, x, y, :, cols]
                        pd, ld = dirg[y, z, x, :, cols], diru[y, z, x, :, cols]
                        b = back[x, y, z, :, cols]
                        s = jax.nn.sigmoid(p)
                        one = s * (1.0 + p * (1.0 - s))
                        two = s * (1.0 - s) * (2.0 + p * (1.0 - 2.0 * s))
                        part[dz, dx, dy] = (b * (ld * one + l * two * pd), b * one * pd)

            def put(a, hi, lo, inner, pair):
                at_row = pl.multiple_of(128 * hi + 32 * lo + 16 * inner, 16)
                for which in range(2):
                    value = jnp.concatenate([v[which] for v in pair], axis=0).astype(BF)
                    parts[a, which, pl.ds(at_row, 16), cols] = value

            for u in range(2):
                for w in range(2):
                    put(0, 2 * zp + u, 2 * xp + w, yp, (part[u, w, 0], part[u, w, 1]))
                    put(1, 2 * yp + u, 2 * zp + w, xp, (part[w, 0, u], part[w, 1, u]))
                    put(2, 2 * xp + u, 2 * yp + w, zp, (part[0, u, w], part[1, u, w]))

    replied = []

    def reply(j):
        for a in range(3):
            f0, f = SPANS[a]
            out = replies[a]
            if j == 1:
                wire.sent(fourth[a][0][0], out.at[pl.ds(0, 3)])
                replied[a].wait()
            done = 0
            while done < f:
                n = min(256, f - done)
                rows = pl.ds(f0 + done, n)
                got = lax.dot_general(parts[a, 0], wg[j, rows, :], NT, preferred_element_type=F32)
                got += lax.dot_general(parts[a, 1], wu[j, rows, :], NT, preferred_element_type=F32)
                out[:, :, :, done : done + n] = got.astype(BF).reshape(4, 4, 32, n)
                done += n
            n3, dim = place.at[ORDERS[a][2]], ORDERS[a][2]
            sent, early, late = fourth[a][j]
            far = mod4(n3 + 2)
            wire.go(sent, early, out.at[far, pl.ds(0, 2)], passing[a].at[j, 0], dim, 1)
            wire.go(sent, early, out.at[far, pl.ds(2, 2)], passing[a].at[j, 1], dim, 3)
            wire.go(sent, late, out.at[mod4(n3 + 1)], backs[a].at[:, n3, j], dim, 1)
            wire.go(sent, late, out.at[mod4(n3 + 3)], backs[a].at[:, n3, j], dim, 3)
            replied.append(copy(out.at[n3], backs[a].at[:, n3, j], 29 + 3 * j + a))

    def replays(j):
        for a in range(3):
            n3, dim = place.at[ORDERS[a][2]], ORDERS[a][2]
            hold = passing[a]
            _, early, late = fourth[a][j]
            wire.got(early, hold.at[j])
            wire.go(repassed[a], late, hold.at[j, 0], backs[a].at[pl.ds(0, 2), mod4(n3 + 3), j], dim, 1)
            wire.go(repassed[a], late, hold.at[j, 1], backs[a].at[pl.ds(2, 2), mod4(n3 + 1), j], dim, 3)

    for a in range(3):
        wire.got(mk2[a][1], meta.at[a, pl.ds(0, 3)])
    for b in (1, 2):
        for a in range(3):
            pass_on(a, ORDERS[a][1], second[a][b], *views2(a, b))
            weigh(a, 2 * b - 2)
            weigh(a, 2 * b - 1)
        if b == 1:
            pack(0)
    for a in range(3):
        pass_on(a, ORDERS[a][1], second[a][3], *views2(a, 3))
    for a in range(3):
        wire.got(second[a][0][2], held.at[a, 0])
    pack(1)
    direct(0)
    relays(0)
    pack(2)
    direct(1)
    relays(1)
    for a in range(3):
        wire.got(second[a][0][3], held.at[a, 0])
    pack(3)
    direct(2)
    relays(2)
    for c in heavy:
        c.wait()
    fetch(0)
    pack(4)
    direct(3)
    relays(3)
    fetch(1)
    layer(0, (0, 1, 2))
    pack(5)
    direct(4)
    relays(4)
    fetch(2)
    fetch(3)
    layer(2, (0,))
    pack(6)
    direct(5)
    relays(5)
    layer(2, (1, 2))
    pack(7)
    direct(6)
    relays(6)
    mix()
    direct(7)
    relays(7)
    fetch(4)
    fetch(5)
    layer(4, (0, 1, 2))
    reply(0)
    fetch(6)
    fetch(7)
    replays(0)
    layer(6, (0, 1, 2))
    mix()
    reply(1)
    replays(1)
    for a in range(3):
        for j in range(2):
            wire.got(fourth[a][j][2], backs[a].at[pl.ds(0, 3), :, j])
        wire.sent(first[a][4], held.at[a, 0, pl.ds(0, 3)])
        wire.sent(second[a][0][4], held.at[a, pl.ds(0, 3)])
        wire.sent(mk1[a][0], meta.at[a, 0, pl.ds(0, 3)])
        wire.sent(mk2[a][0], meta.at[a, pl.ds(0, 3)])
        for s in (5, 6, 7):
            wire.sent(third[a][s][0], packed.at[a, 0, pl.ds(0, 3)])
        wire.sent(passed[a], relay.at[a])
        wire.sent(fourth[a][1][0], replies[a].at[pl.ds(0, 3)])
        wire.sent(repassed[a], passing[a])
    for c in replied[3:] + stored[-2:]:
        c.wait()


N_GROUPS, N_TAKEN, N_LOCAL = 6 + 6 + 30 + 6, 42 + 6 + 48 + 12, 35
SPANS = ((0, 768), (768, 640), (1408, 640))


def dispatch(tok, tan, adj, ids, gates, wg, wu, wd):
    vmem = pl.BlockSpec(memory_space=pltpu.VMEM)
    hbm = pl.BlockSpec(memory_space=pl.ANY)
    rows = jax.ShapeDtypeStruct((2, 4, 4, 32, D), BF)
    out = pl.pallas_call(
        dispatch_kernel,
        out_shape=(rows, rows, rows)
        + tuple(jax.ShapeDtypeStruct((4, 4, 2, 32, f), BF) for _, f in SPANS)
        + (jax.ShapeDtypeStruct((3, 4, 2, 256, 256), BF),),
        in_specs=[hbm] * 3 + [vmem] * 2 + [hbm] * 3,
        out_specs=(hbm,) * 7,
        scratch_shapes=[
            pltpu.VMEM((3, 4, 4, TOK, D), BF),
            pltpu.VMEM((3, 3, 4, 32, D), BF),
            pltpu.VMEM((3, 8, 2, 16, D), BF),
            pltpu.VMEM((3, 4, 4, 8, 128), F32),
            pltpu.VMEM((3, 4, 4, 32, D), BF),
            pltpu.VMEM((2, D, FF), BF),
            pltpu.VMEM((2, D, FF), BF),
            pltpu.VMEM((2, FF, D), BF),
        ]
        + [pltpu.VMEM((4, 4, 4, 8, FF), F32)] * 5
        + [pltpu.VMEM((3, 2, 512, FF), BF)]
        + [pltpu.VMEM((4, 4, 32, f), BF) for _, f in SPANS]
        + [pltpu.VMEM((2, 2, 2, 32, f), BF) for _, f in SPANS]
        + [
            pltpu.VMEM((3, 4, 2, 128, 256), BF),
            pltpu.VMEM((256, 256), F32),
            pltpu.VMEM((2, 2, 256, 256), BF),
            pltpu.SemaphoreType.DMA((N_GROUPS,)),
            pltpu.SemaphoreType.DMA((N_TAKEN,)),
            pltpu.SemaphoreType.DMA((N_LOCAL,)),
        ],
        compiler_params=pltpu.CompilerParams(
            collective_id=1, has_side_effects=True, vmem_limit_bytes=67043328
        ),
        name="dispatch",
    )(tok, tan, adj, ids, gates, wg, wu, wd)
    return out[3:]


def collect_kernel(b0, b1, b2, grown_in, tan, hvp, ratio, *scratch):
    place = Place()
    n_part = 8
    parts = [scratch[i * n_part : (i + 1) * n_part] for i in range(9)]
    grown, plane, line, send, recv, local = scratch[9 * n_part :]
    wire = Wire(place, send, recv)
    spots = iter(range(12))
    backs = (b0, b1, b2)

    def copy(src, dst):
        c = pltpu.make_async_copy(src, dst, local.at[next(spots)])
        c.start()
        return c

    loads = {}
    for q in range(3):
        for a, f0, n in PARTS[q]:
            loads[q, a] = copy(backs[a].at[:, :, :, pl.ds(f0 - SPANS[a][0], n)], parts[3 * q + a][0])
            if q == 0:
                loads[a] = copy(grown_in.at[a], grown.at[a])
    y, x, z = place.at
    near = [(place.dp, lax.rem(y + i // 4, 4) * 16 + lax.rem(x + i % 4, 4) * 4 + z) for i in range(1, 16)]
    tall = [(lax.rem(place.dp + i // 4, 2), place.shifted(2, i % 4)) for i in range(1, 8)]
    sem = pltpu.get_barrier_semaphore()
    for other in near + tall:
        pl.semaphore_signal(sem, inc=1, device_id=other, device_id_type=MESH)
    pl.semaphore_wait(sem, 22)
    keys = [[[wire.group(), wire.group()] + [wire.take() for _ in range(6)] for _ in range(3)] for _ in range(3)]
    at = [tuple(place.at[d] for d in ORDERS[a]) for a in range(3)]
    state = {"square": jnp.zeros((8, 128), F32)}

    def total(q, a, r):
        n = PARTS[q][a][2]
        rows = parts[3 * q + a][0][mod4(at[a][1] + r)].reshape(256, n)
        got = jnp.dot(grown[a, r, 0], rows, preferred_element_type=F32)
        got = got + jnp.dot(grown[a, r, 1], rows, preferred_element_type=F32)
        return got.reshape(4, 64, n)

    def far2(q):
        for a, _, n in PARTS[q]:
            own, out2, mid2 = parts[3 * q + a][1:4]
            dim = ORDERS[a][1]
            k = keys[q][a]
            loads[q, a].wait()
            if q == 0:
                loads[a].wait()
            out2[...] = total(q, a, 2).astype(BF)
            wire.go(k[0], k[2], out2.at[pl.ds(0, 2)], mid2.at[0], dim, 1)
            wire.go(k[0], k[3], out2.at[pl.ds(2, 2)], mid2.at[1], dim, 3)
        for a, _, n in PARTS[q]:
            parts[3 * q + a][1][...] = total(q, a, 0)

    def near2(q):
        for a, _, n in PARTS[q]:
            mid2, to2, in2 = parts[3 * q + a][3:6]
            k, dim = keys[q][a], ORDERS[a][1]
            for side, r in ((0, 1), (1, 3)):
                got = total(q, a, r)
                wire.got(k[2 + side], mid2.at[side])
                came = mid2[side].astype(F32)
                lo, hi = got[0:2], got[2:4]
                if side == 0:
                    lo = lo + came
                else:
                    hi = hi + came
                to2[side, 0:2] = lo.astype(BF)
                to2[side, 2:4] = hi.astype(BF)
                wire.go(k[0], k[4], to2.at[side], in2.at[side], dim, r)

    def far1(q):
        for a, _, n in PARTS[q]:
            own, in2, out1, mid1 = (parts[3 * q + a][i] for i in (1, 5, 6, 7))
            n1, dim = at[a][0], ORDERS[a][0]
            k = keys[q][a]
            wire.got(k[4], in2)
            own[...] = own[...] + (in2[0].astype(F32) + in2[1].astype(F32))
            out1[0] = own[mod4(n1 + 2)].astype(BF)
            wire.go(k[1], k[5], out1.at[0, pl.ds(0, 32)], mid1.at[0, pl.ds(0, 32)], dim, 1)
            wire.go(k[1], k[6], out1.at[0, pl.ds(32, 32)], mid1.at[0, pl.ds(32, 32)], dim, 3)

    def near1(q):
        for a, _, n in PARTS[q]:
            own, in2, out1, mid1 = (parts[3 * q + a][i] for i in (1, 5, 6, 7))
            n1, dim = at[a][0], ORDERS[a][0]
            k = keys[q][a]
            for side, r in ((0, 1), (1, 3)):
                rows = pl.ds(32 * side, 32)
                rest = pl.ds(32 - 32 * side, 32)
                wire.got(k[5 + side], mid1.at[0, rows])
                s = mod4(n1 + r)
                out1[1 + side, rows] = (own[s, rows] + mid1[0, rows].astype(F32)).astype(BF)
                out1[1 + side, rest] = own[s, rest].astype(BF)
                wire.go(k[1], k[7], out1.at[1 + side], mid1.at[1 + side], dim, r)

    def finish(q):
        for a, f0, n in PARTS[q]:
            own, mid1 = parts[3 * q + a][1], parts[3 * q + a][7]
            k = keys[q][a]
            wire.got(k[7], mid1.at[pl.ds(1, 2)])
            got = own[at[a][0]] + (mid1[1].astype(F32) + mid1[2].astype(F32))
            hvp[:, f0 : f0 + n] = got
            state["square"] += jnp.sum((got * got).reshape(8, 8, n // 128, 128), axis=(0, 2))

    far2(0)
    far2(1)
    near2(0)
    far2(2)
    far1(0)
    near2(1)
    near1(0)
    t = tan[...].astype(F32)
    low = jnp.sum((t * t).reshape(8, 8, 16, 128), axis=(0, 2))
    far1(1)
    near2(2)
    finish(0)
    near1(1)
    far1(2)
    finish(1)
    near1(2)
    finish(2)

    def share(table, value, spot, others):
        table[spot, 0] = value[0]
        table[spot, 1] = value[1]
        sent, came = wire.group(), wire.take()
        for other in others:
            wire.push(sent, came, table.at[spot], table.at[spot], other)
        wire.got(came, table.at[pl.ds(0, len(others))])
        wire.sent(sent, table.at[pl.ds(0, len(others))])
        return jnp.sum(table[...], axis=0)

    full = share(plane, (state["square"], low), y * 4 + x, near)
    full = share(line, (full[0], full[1]), place.dp * 4 + z, tall)
    top, low = jnp.sum(full[0]), jnp.sum(full[1])
    ratio[...] = jnp.full((8, 128), top, F32) / jnp.full((8, 128), low, F32)
    for q in range(3):
        for a in range(3):
            back, _, _, _, _, _, out1, _ = parts[3 * q + a]
            wire.sent(keys[q][a][0], back.at[pl.ds(0, 3)])
            wire.sent(keys[q][a][1], out1)


N_SENT, N_CAME = 18 + 2, 54 + 2


def collect(backs, grown, tan):
    vmem = pl.BlockSpec(memory_space=pltpu.VMEM)
    hbm = pl.BlockSpec(memory_space=pl.ANY)
    scratch = []
    for q in range(3):
        for _, _, f in PARTS[q]:
            scratch += [
                pltpu.VMEM((4, 4, 64, f), BF),
                pltpu.VMEM((4, 64, f), F32),
                pltpu.VMEM((4, 64, f), BF),
                pltpu.VMEM((2, 2, 64, f), BF),
                pltpu.VMEM((2, 4, 64, f), BF),
                pltpu.VMEM((2, 4, 64, f), BF),
                pltpu.VMEM((3, 64, f), BF),
                pltpu.VMEM((3, 64, f), BF),
            ]
    scratch += [
        pltpu.VMEM((3, 4, 2, 256, 256), BF),
        pltpu.VMEM((16, 2, 8, 128), F32),
        pltpu.VMEM((8, 2, 8, 128), F32),
        pltpu.SemaphoreType.DMA((N_SENT,)),
        pltpu.SemaphoreType.DMA((N_CAME,)),
        pltpu.SemaphoreType.DMA((12,)),
    ]
    return pl.pallas_call(
        collect_kernel,
        out_shape=(jax.ShapeDtypeStruct((TOK, D), F32), jax.ShapeDtypeStruct((8, 128), F32)),
        in_specs=[hbm] * 4 + [vmem],
        out_specs=(vmem, vmem),
        scratch_shapes=scratch,
        compiler_params=pltpu.CompilerParams(
            collective_id=2, has_side_effects=True, vmem_limit_bytes=67043328
        ),
        name="collect",
    )(*backs, grown, tan)


def local(tokens, tangent, adjoint, gates, expert_ids, w_gate, w_up, w_down):
    *backs, grown = dispatch(tokens, tangent, adjoint, expert_ids.T, gates.T, w_gate, w_up, w_down)
    backs = [b.reshape(4, 4, 64, b.shape[-1]) for b in backs]
    hvp, ratio = collect(backs, grown, tangent)
    return hvp, ratio[0, 0]


def solution(mesh):
    rows = P(("dp", "expert"), None)
    weights = P("expert", None, None)
    return jax.shard_map(
        local,
        mesh=mesh,
        in_specs=(rows,) * 5 + (weights,) * 3,
        out_specs=(rows, P()),
        check_vma=False,
    )
```

time: 200 us -> 182 us (0.910)
  Pallas kernels: 194 us -> 178 us
  local copies, waits for them, and re-layouts: 5.83 us -> 3.07 us
    pallas_call x1, Pallas kernels: 68 us -> 49.1 us  [collect(): pl.pallas_call(collect_kernel, out_shape=(jax.ShapeDtypeStruct((TOK, D),...]
    pallas_call x1, Pallas kernels: 126 us -> 129 us  [dispatch(): pl.pallas_call(dispatch_kernel, out_shape=(rows, rows, rows) + tuple((jax...]
    unnamed x3 -> x1, local copies, waits for them, and re-layouts: 4.65 us -> 1.87 us
where the time goes in v2:
time: 182 us; the launch traced here: 181 us
  Pallas kernels  178 us (98%)
  local copies, waits for them, and re-layouts  3.07 us (2%)
    pallas_call x1, Pallas kernels, dispatch(): pl.pallas_call(dispatch_kernel, out_shape=(rows, rows, rows) + tuple((jax...  129 us
    pallas_call x1, Pallas kernels, collect(): pl.pallas_call(collect_kernel, out_shape=(jax.ShapeDtypeStruct((TOK, D),...  49.1 us

profile of v2, /device:TPU:1, one launch (start us, length us, event | category | flops | bytes accessed | tf_op | source)
XLA Modules:
  0.0 181.4 jit_solution(13969255783177867785)
XLA Ops:
  0.6 128.6 %dispatch.1 = (bf16[2,4,4,32,2048]{4,3,2,1,0:T(8,128)(2,1)}, bf16[2,4,4,32,2048]{4,3,2,1,0:T(8,128)(2,1)}, bf16[2,4,4,32,2048]{4,3,2,1,0:T(8,128)(2,1)}, bf16[4,...) custom-call(bf16[64,2048]{1,0:T(8,128)(2,1)} %tok.1, ...), custom_call_target="tpu_custom_call" | custom-call | tf_op jit(solution)/shard_map/dispatch/pallas_call | solution.py:452
  129.2 49.1 %collect.1 = (f32[64,2048]{1,0:T(8,128)}, f32[8,128]{1,0:T(8,128)}) custom-call(bf16[4,4,64,768]{3,2,1,0:T(8,128)(2,1)} %bitcast.6, bf16[4,4,64,640]{3,2,1,0:T(8,128)(2,1)} %bitcast.7, bf16[4,4,64,640]{3,2,1,0:T(8,128)(2,1)} %bitcast.8, bf16[3,4,2,256,256]{4,3,2,1,0:T(8,128)(2,1)} %get-tuple-element.11.grown_in, bf16[64,2048]{1,0:T(8,128)(2,1)} %tan.3), custom_call_target="tpu_custom_call" | custom-call | tf_op jit(solution)/shard_map/collect/pallas_call | solution.py:658
  178.3 1.2 slice.3
  179.5 1.9 %copy.11 = f32[64,2048]{1,0:T(8,128)} copy(f32[64,2048]{1,0:T(8,128)} %get-tuple-element.16) | data formatting | bytes 1048576

commit v3 on v2

--- a/solution.py
+++ b/solution.py
@@ -200,15 +200,13 @@
         for e in range(8):
             spin[pl.ds(32 * e, 32), :] = jnp.where(index[e : e + 1, :] == slots, weight[e : e + 1, :], 0.0)
         w = spin[...].T
-        high = w.astype(BF)
         for e in range(8):
             hit = jnp.where(index[e : e + 1, :] == slots, 1.0, 0.0)
             picks[a, r, e % 2, pl.ds(32 * (e // 2), 32), :] = hit.astype(BF)
         n = len(stored)
         if n >= 2:
             stored[n - 2].wait()
-        grow[n % 2, 0] = high
-        grow[n % 2, 1] = (w - high.astype(F32)).astype(BF)
+        grow[n % 2] = w.astype(BF)
         stored.append(copy(grow.at[n % 2], grown.at[a, r], 6 + n % 2))
 
     third = [[(wire.group(), wire.take(), wire.take()) for _ in range(8)] for _ in range(3)]
@@ -392,27 +390,26 @@
     relays(2)
     for c in heavy:
         c.wait()
-    fetch(0)
     pack(4)
     direct(3)
     relays(3)
-    fetch(1)
-    layer(0, (0, 1, 2))
+    fetch(0)
     pack(5)
     direct(4)
     relays(4)
-    fetch(2)
-    fetch(3)
-    layer(2, (0,))
+    fetch(1)
+    layer(0, (0, 1, 2))
     pack(6)
     direct(5)
     relays(5)
-    layer(2, (1, 2))
+    fetch(2)
+    fetch(3)
+    layer(2, (0, 1, 2))
     pack(7)
     direct(6)
     relays(6)
+    direct(7)
     mix()
-    direct(7)
     relays(7)
     fetch(4)
     fetch(5)
@@ -453,7 +450,7 @@
         dispatch_kernel,
         out_shape=(rows, rows, rows)
         + tuple(jax.ShapeDtypeStruct((4, 4, 2, 32, f), BF) for _, f in SPANS)
-        + (jax.ShapeDtypeStruct((3, 4, 2, 256, 256), BF),),
+        + (jax.ShapeDtypeStruct((3, 4, 256, 256), BF),),
         in_specs=[hbm] * 3 + [vmem] * 2 + [hbm] * 3,
         out_specs=(hbm,) * 7,
         scratch_shapes=[
@@ -473,7 +470,7 @@
         + [
             pltpu.VMEM((3, 4, 2, 128, 256), BF),
             pltpu.VMEM((256, 256), F32),
-            pltpu.VMEM((2, 2, 256, 256), BF),
+            pltpu.VMEM((2, 256, 256), BF),
             pltpu.SemaphoreType.DMA((N_GROUPS,)),
             pltpu.SemaphoreType.DMA((N_TAKEN,)),
             pltpu.SemaphoreType.DMA((N_LOCAL,)),
@@ -520,8 +517,7 @@
     def total(q, a, r):
         n = PARTS[q][a][2]
         rows = parts[3 * q + a][0][mod4(at[a][1] + r)].reshape(256, n)
-        got = jnp.dot(grown[a, r, 0], rows, preferred_element_type=F32)
-        got = got + jnp.dot(grown[a, r, 1], rows, preferred_element_type=F32)
+        got = jnp.dot(grown[a, r], rows, preferred_element_type=F32)
         return got.reshape(4, 64, n)
 
     def far2(q):
@@ -620,7 +616,7 @@
     full = share(plane, (state["square"], low), y * 4 + x, near)
     full = share(line, (full[0], full[1]), place.dp * 4 + z, tall)
     top, low = jnp.sum(full[0]), jnp.sum(full[1])
-    ratio[...] = jnp.full((8, 128), top, F32) / jnp.full((8, 128), low, F32)
+    ratio[...] = jnp.full((1, 1), top, F32) / jnp.full((1, 1), low, F32)
     for q in range(3):
         for a in range(3):
             back, _, _, _, _, _, out1, _ = parts[3 * q + a]
@@ -648,7 +644,7 @@
                 pltpu.VMEM((3, 64, f), BF),
             ]
     scratch += [
-        pltpu.VMEM((3, 4, 2, 256, 256), BF),
+        pltpu.VMEM((3, 4, 256, 256), BF),
         pltpu.VMEM((16, 2, 8, 128), F32),
         pltpu.VMEM((8, 2, 8, 128), F32),
         pltpu.SemaphoreType.DMA((N_SENT,)),
@@ -657,12 +653,12 @@
     ]
     return pl.pallas_call(
         collect_kernel,
-        out_shape=(jax.ShapeDtypeStruct((TOK, D), F32), jax.ShapeDtypeStruct((8, 128), F32)),
+        out_shape=(jax.ShapeDtypeStruct((TOK, D), F32), jax.ShapeDtypeStruct((1, 1), F32)),
         in_specs=[hbm] * 4 + [vmem],
         out_specs=(vmem, vmem),
         scratch_shapes=scratch,
         compiler_params=pltpu.CompilerParams(
-            collective_id=2, has_side_effects=True, vmem_limit_bytes=67043328
+            collective_id=2, has_side_effects=True, vmem_limit_bytes=64100000
         ),
         name="collect",
     )(*backs, grown, tan)

time: 182 us -> 184 us (1.011)
  Pallas kernels: 178 us -> 180 us
    pallas_call x1, Pallas kernels: 129 us -> 131 us  [dispatch(): pl.pallas_call(dispatch_kernel, out_shape=(rows, rows, rows) + tuple((jax...]
where the time goes in v3:
time: 184 us
  Pallas kernels  180 us (98%)
  between operations  2.41 us (1%)
  local copies, waits for them, and re-layouts  1.87 us (1%)
    pallas_call x1, Pallas kernels, dispatch(): pl.pallas_call(dispatch_kernel, out_shape=(rows, rows, rows) + tuple((jax...  131 us
    pallas_call x1, Pallas kernels, collect(): pl.pallas_call(collect_kernel, out_shape=(jax.ShapeDtypeStruct((TOK, D),...  48.7 us

profile of v3, /device:TPU:1, one launch (start us, length us, event | category | flops | bytes accessed | tf_op | source)
XLA Modules:
  0.0 184.1 jit_solution(13369622982600778093)
XLA Ops:
  0.6 131.1 %dispatch.1 = (bf16[2,4,4,32,2048]{4,3,2,1,0:T(8,128)(2,1)}, bf16[2,4,4,32,2048]{4,3,2,1,0:T(8,128)(2,1)}, bf16[2,4,4,32,2048]{4,3,2,1,0:T(8,128)(2,1)}, bf16[4,...) custom-call(bf16[64,2048]{1,0:T(8,128)(2,1)} %tok.1, ...), custom_call_target="tpu_custom_call" | custom-call | tf_op jit(solution)/shard_map/dispatch/pallas_call | solution.py:449
  131.7 48.7 %collect.1 = (f32[64,2048]{1,0:T(8,128)}, f32[1,1]{1,0:T(1,128)}) custom-call(bf16[4,4,64,768]{3,2,1,0:T(8,128)(2,1)} %bitcast.6, bf16[4,4,64,640]{3,2,1,0:T(8,128)(2,1)} %bitcast.7, bf16[4,4,64,640]{3,2,1,0:T(8,128)(2,1)} %bitcast.8, bf16[3,4,256,256]{3,2,1,0:T(8,128)(2,1)} %get-tuple-element.11.grown_in, bf16[64,2048]{1,0:T(8,128)(2,1)} %tan.3), custom_call_target="tpu_custom_call" | custom-call | tf_op jit(solution)/shard_map/collect/pallas_call | solution.py:654
  180.4 1.9 %copy.12 = f32[64,2048]{1,0:T(8,128)} copy(f32[64,2048]{1,0:T(8,128)} %get-tuple-element.16) | data formatting | bytes 1048576

commit v4 on v2

--- a/solution.py
+++ b/solution.py
@@ -118,7 +118,7 @@
         return c
 
     own = [copy(src, held.at[a, at[a][0], at[a][1]], a) for a, src in enumerate((tok, tan, adj))]
-    heavy = [copy(wg_in, wg, 3), copy(wu_in, wu, 4), copy(wd_in, wd, 5)]
+    heavy = [copy(wg_in, wg, 3), copy(wu_in, wu, 4), copy(wd_in, chunk, 5)]
     turned = jnp.concatenate([ids[...].astype(F32), gates[...]], axis=1)
     for a in range(3):
         meta[a, at[a][0], at[a][1]] = turned
@@ -212,7 +212,7 @@
         stored.append(copy(grow.at[n % 2], grown.at[a, r], 6 + n % 2))
 
     third = [[(wire.group(), wire.take(), wire.take()) for _ in range(8)] for _ in range(3)]
-    fourth = [[(wire.group(), wire.take(), wire.take()) for _ in range(2)] for _ in range(3)]
+    fourth = [[(wire.group(), [wire.take() for _ in range(3)], wire.take()) for _ in range(2)] for _ in range(3)]
     passed = [wire.group() for _ in range(3)]
     repassed = [wire.group() for _ in range(3)]
     kept = {}
@@ -294,7 +294,7 @@
                         ref[:, spots2[i], :, :, cols] = value[i]
 
                 if a == 2:
-                    put(back, lax.dot_general(rows, wd[j, cols, :], NT, preferred_element_type=F32))
+                    put(back, jnp.dot(rows, wd[j, :, cols], preferred_element_type=F32))
                 else:
                     x, y = (pre, lin) if a == 0 else (dirg, diru)
                     put(x, jnp.dot(rows, wg[j, :, cols], preferred_element_type=F32))
@@ -334,45 +334,61 @@
     replied = []
 
     def reply(j):
-        for a in range(3):
-            f0, f = SPANS[a]
-            out = replies[a]
-            if j == 1:
-                wire.sent(fourth[a][0][0], out.at[pl.ds(0, 3)])
-                replied[a].wait()
-            done = 0
-            while done < f:
-                n = min(256, f - done)
-                rows = pl.ds(f0 + done, n)
+        for c, pieces in enumerate(PARTS):
+            for a, start, n in pieces:
+                f0, f = SPANS[a]
+                out = replies[a]
+                if j == 1 and c == 0:
+                    wire.sent(fourth[a][0][0], out.at[pl.ds(0, 3)])
+                    replied[a].wait()
+                rows = pl.ds(start, n)
                 got = lax.dot_general(parts[a, 0], wg[j, rows, :], NT, preferred_element_type=F32)
                 got += lax.dot_general(parts[a, 1], wu[j, rows, :], NT, preferred_element_type=F32)
-                out[:, :, :, done : done + n] = got.astype(BF).reshape(4, 4, 32, n)
-                done += n
-            n3, dim = place.at[ORDERS[a][2]], ORDERS[a][2]
-            sent, early, late = fourth[a][j]
-            far = mod4(n3 + 2)
-            wire.go(sent, early, out.at[far, pl.ds(0, 2)], passing[a].at[j, 0], dim, 1)
-            wire.go(sent, early, out.at[far, pl.ds(2, 2)], passing[a].at[j, 1], dim, 3)
-            wire.go(sent, late, out.at[mod4(n3 + 1)], backs[a].at[:, n3, j], dim, 1)
-            wire.go(sent, late, out.at[mod4(n3 + 3)], backs[a].at[:, n3, j], dim, 3)
-            replied.append(copy(out.at[n3], backs[a].at[:, n3, j], 29 + 3 * j + a))
+                cols = pl.ds(start - f0, n)
+                out[:, :, :, cols] = got.astype(BF).reshape(4, 4, 32, n)
+                n3, dim = place.at[ORDERS[a][2]], ORDERS[a][2]
+                sent, early, late = fourth[a][j]
+                far = mod4(n3 + 2)
+                here = out.at[:, :, :, cols]
+                there = backs[a].at[:, n3, j, :, cols]
+                hold = passing[a].at[j, :, :, :, cols]
+                wire.go(sent, early[c], here.at[far, pl.ds(0, 2)], hold.at[0], dim, 1)
+                wire.go(sent, early[c], here.at[far, pl.ds(2, 2)], hold.at[1], dim, 3)
+                wire.go(sent, late, here.at[mod4(n3 + 1)], there, dim, 1)
+                wire.go(sent, late, here.at[mod4(n3 + 3)], there, dim, 3)
+                if c == 2:
+                    replied.append(copy(out.at[n3], backs[a].at[:, n3, j], 29 + 3 * j + a))
 
     def replays(j):
-        for a in range(3):
-            n3, dim = place.at[ORDERS[a][2]], ORDERS[a][2]
-            hold = passing[a]
-            _, early, late = fourth[a][j]
-            wire.got(early, hold.at[j])
-            wire.go(repassed[a], late, hold.at[j, 0], backs[a].at[pl.ds(0, 2), mod4(n3 + 3), j], dim, 1)
-            wire.go(repassed[a], late, hold.at[j, 1], backs[a].at[pl.ds(2, 2), mod4(n3 + 1), j], dim, 3)
+        for c, pieces in enumerate(PARTS):
+            for a, start, n in pieces:
+                n3, dim = place.at[ORDERS[a][2]], ORDERS[a][2]
+                cols = pl.ds(start - SPANS[a][0], n)
+                hold = passing[a].at[j, :, :, :, cols]
+                _, early, late = fourth[a][j]
+                wire.got(early[c], hold)
+                there = backs[a].at[:, :, j, :, cols]
+                wire.go(repassed[a], late, hold.at[0], there.at[pl.ds(0, 2), mod4(n3 + 3)], dim, 1)
+                wire.go(repassed[a], late, hold.at[1], there.at[pl.ds(2, 2), mod4(n3 + 1)], dim, 3)
 
     for a in range(3):
         wire.got(mk2[a][1], meta.at[a, pl.ds(0, 3)])
+    def turn_over(k):
+        if k == 0:
+            heavy[2].wait()
+
+        @pl.loop(0, 8)
+        def _(m):
+            cols = pl.ds(pl.multiple_of(m * 256, 256), 256)
+            block = chunk[k // 2, 2 * (k % 2) : 2 * (k % 2) + 2, :, :, cols].reshape(256, 256)
+            wd[k // 3, cols, 256 * (k % 3) : 256 * (k % 3) + 256] = block.T
+
     for b in (1, 2):
         for a in range(3):
             pass_on(a, ORDERS[a][1], second[a][b], *views2(a, b))
             weigh(a, 2 * b - 2)
             weigh(a, 2 * b - 1)
+            turn_over(3 * b - 3 + a)
         if b == 1:
             pack(0)
     for a in range(3):
@@ -390,8 +406,8 @@
     pack(3)
     direct(2)
     relays(2)
-    for c in heavy:
-        c.wait()
+    heavy[0].wait()
+    heavy[1].wait()
     fetch(0)
     pack(4)
     direct(3)
@@ -411,8 +427,8 @@
     pack(7)
     direct(6)
     relays(6)
+    direct(7)
     mix()
-    direct(7)
     relays(7)
     fetch(4)
     fetch(5)
@@ -441,7 +457,7 @@
         c.wait()
 
 
-N_GROUPS, N_TAKEN, N_LOCAL = 6 + 6 + 30 + 6, 42 + 6 + 48 + 12, 35
+N_GROUPS, N_TAKEN, N_LOCAL = 6 + 6 + 30 + 6, 42 + 6 + 48 + 24, 35
 SPANS = ((0, 768), (768, 640), (1408, 640))
 
 
@@ -464,7 +480,7 @@
             pltpu.VMEM((3, 4, 4, 32, D), BF),
             pltpu.VMEM((2, D, FF), BF),
             pltpu.VMEM((2, D, FF), BF),
-            pltpu.VMEM((2, FF, D), BF),
+            pltpu.VMEM((2, D, FF), BF),
         ]
         + [pltpu.VMEM((4, 4, 4, 8, FF), F32)] * 5
         + [pltpu.VMEM((3, 2, 512, FF), BF)]
@@ -513,7 +529,7 @@
     for other in near + tall:
         pl.semaphore_signal(sem, inc=1, device_id=other, device_id_type=MESH)
     pl.semaphore_wait(sem, 22)
-    keys = [[[wire.group(), wire.group()] + [wire.take() for _ in range(6)] for _ in range(3)] for _ in range(3)]
+    keys = [[[wire.group(), wire.group()] + [wire.take() for _ in range(4)] for _ in range(3)] for _ in range(3)]
     at = [tuple(place.at[d] for d in ORDERS[a]) for a in range(3)]
     state = {"square": jnp.zeros((8, 128), F32)}
 
@@ -555,37 +571,23 @@
                 to2[side, 2:4] = hi.astype(BF)
                 wire.go(k[0], k[4], to2.at[side], in2.at[side], dim, r)
 
-    def far1(q):
+    def last(q):
         for a, _, n in PARTS[q]:
             own, in2, out1, mid1 = (parts[3 * q + a][i] for i in (1, 5, 6, 7))
             n1, dim = at[a][0], ORDERS[a][0]
             k = keys[q][a]
             wire.got(k[4], in2)
             own[...] = own[...] + (in2[0].astype(F32) + in2[1].astype(F32))
-            out1[0] = own[mod4(n1 + 2)].astype(BF)
-            wire.go(k[1], k[5], out1.at[0, pl.ds(0, 32)], mid1.at[0, pl.ds(0, 32)], dim, 1)
-            wire.go(k[1], k[6], out1.at[0, pl.ds(32, 32)], mid1.at[0, pl.ds(32, 32)], dim, 3)
-
-    def near1(q):
-        for a, _, n in PARTS[q]:
-            own, in2, out1, mid1 = (parts[3 * q + a][i] for i in (1, 5, 6, 7))
-            n1, dim = at[a][0], ORDERS[a][0]
-            k = keys[q][a]
-            for side, r in ((0, 1), (1, 3)):
-                rows = pl.ds(32 * side, 32)
-                rest = pl.ds(32 - 32 * side, 32)
-                wire.got(k[5 + side], mid1.at[0, rows])
-                s = mod4(n1 + r)
-                out1[1 + side, rows] = (own[s, rows] + mid1[0, rows].astype(F32)).astype(BF)
-                out1[1 + side, rest] = own[s, rest].astype(BF)
-                wire.go(k[1], k[7], out1.at[1 + side], mid1.at[1 + side], dim, r)
+            for by in (2, 1, 3):
+                out1[by - 1] = own[mod4(n1 + by)].astype(BF)
+                wire.go(k[1], k[5], out1.at[by - 1], mid1.at[by - 1], dim, by)
 
     def finish(q):
         for a, f0, n in PARTS[q]:
             own, mid1 = parts[3 * q + a][1], parts[3 * q + a][7]
             k = keys[q][a]
-            wire.got(k[7], mid1.at[pl.ds(1, 2)])
-            got = own[at[a][0]] + (mid1[1].astype(F32) + mid1[2].astype(F32))
+            wire.got(k[5], mid1)
+            got = own[at[a][0]] + (mid1[0].astype(F32) + mid1[1].astype(F32) + mid1[2].astype(F32))
             hvp[:, f0 : f0 + n] = got
             state["square"] += jnp.sum((got * got).reshape(8, 8, n // 128, 128), axis=(0, 2))
 
@@ -593,18 +595,15 @@
     far2(1)
     near2(0)
     far2(2)
-    far1(0)
+    last(0)
     near2(1)
-    near1(0)
     t = tan[...].astype(F32)
     low = jnp.sum((t * t).reshape(8, 8, 16, 128), axis=(0, 2))
-    far1(1)
     near2(2)
     finish(0)
-    near1(1)
-    far1(2)
+    last(1)
     finish(1)
-    near1(2)
+    last(2)
     finish(2)
 
     def share(table, value, spot, others):
@@ -620,7 +619,7 @@
     full = share(plane, (state["square"], low), y * 4 + x, near)
     full = share(line, (full[0], full[1]), place.dp * 4 + z, tall)
     top, low = jnp.sum(full[0]), jnp.sum(full[1])
-    ratio[...] = jnp.full((8, 128), top, F32) / jnp.full((8, 128), low, F32)
+    ratio[...] = jnp.full((1, 1), top, F32) / jnp.full((1, 1), low, F32)
     for q in range(3):
         for a in range(3):
             back, _, _, _, _, _, out1, _ = parts[3 * q + a]
@@ -628,7 +627,7 @@
             wire.sent(keys[q][a][1], out1)
 
 
-N_SENT, N_CAME = 18 + 2, 54 + 2
+N_SENT, N_CAME = 18 + 2, 36 + 2
 
 
 def collect(backs, grown, tan):
@@ -657,7 +656,7 @@
     ]
     return pl.pallas_call(
         collect_kernel,
-        out_shape=(jax.ShapeDtypeStruct((TOK, D), F32), jax.ShapeDtypeStruct((8, 128), F32)),
+        out_shape=(jax.ShapeDtypeStruct((TOK, D), F32), jax.ShapeDtypeStruct((1, 1), F32)),
         in_specs=[hbm] * 4 + [vmem],
         out_specs=(vmem, vmem),
         scratch_shapes=scratch,
@@ -669,6 +668,7 @@
 
 
 def local(tokens, tangent, adjoint, gates, expert_ids, w_gate, w_up, w_down):
+    w_down = w_down.reshape(3, 4, 4, 32, D)
     *backs, grown = dispatch(tokens, tangent, adjoint, expert_ids.T, gates.T, w_gate, w_up, w_down)
     backs = [b.reshape(4, 4, 64, b.shape[-1]) for b in backs]
     hvp, ratio = collect(backs, grown, tangent)

time: 182 us -> 184 us (1.011)
    pallas_call x1, Pallas kernels: 129 us -> 134 us  [dispatch(): pl.pallas_call(dispatch_kernel, out_shape=(rows, rows, rows) + tuple((jax...]
    pallas_call x1, Pallas kernels: 49.1 us -> 45.1 us  [collect(): pl.pallas_call(collect_kernel, out_shape=(jax.ShapeDtypeStruct((TOK, D),...]
where the time goes in v4:
time: 184 us
  Pallas kernels  179 us (97%)
  between operations  2.41 us (1%)
  local copies, waits for them, and re-layouts  1.87 us (1%)
    pallas_call x1, Pallas kernels, dispatch(): pl.pallas_call(dispatch_kernel, out_shape=(rows, rows, rows) + tuple((jax...  134 us
    pallas_call x1, Pallas kernels, collect(): pl.pallas_call(collect_kernel, out_shape=(jax.ShapeDtypeStruct((TOK, D),...  45.1 us

profile of v4, /device:TPU:1, one launch (start us, length us, event | category | flops | bytes accessed | tf_op | source)
XLA Modules:
  0.0 183.6 jit_solution(996900769332232007)
XLA Ops:
  0.6 134.2 %dispatch.1 = (bf16[2,4,4,32,2048]{4,3,2,1,0:T(8,128)(2,1)}, bf16[2,4,4,32,2048]{4,3,2,1,0:T(8,128)(2,1)}, bf16[2,4,4,32,2048]{4,3,2,1,0:T(8,128)(2,1)}, bf16[4,...) custom-call(bf16[64,2048]{1,0:T(8,128)(2,1)} %tok.1, ...), custom_call_target="tpu_custom_call" | custom-call | tf_op jit(solution)/shard_map/dispatch/pallas_call | solution.py:468
  134.8 45.1 %collect.1 = (f32[64,2048]{1,0:T(8,128)}, f32[1,1]{1,0:T(1,128)}) custom-call(bf16[4,4,64,768]{3,2,1,0:T(8,128)(2,1)} %bitcast.8, bf16[4,4,64,640]{3,2,1,0:T(8,128)(2,1)} %bitcast.9, bf16[4,4,64,640]{3,2,1,0:T(8,128)(2,1)} %bitcast.10, bf16[3,4,2,256,256]{4,3,2,1,0:T(8,128)(2,1)} %get-tuple-element.11.grown_in, bf16[64,2048]{1,0:T(8,128)(2,1)} %tan.3), custom_call_target="tpu_custom_call" | custom-call | tf_op jit(solution)/shard_map/collect/pallas_call | solution.py:657
  179.9 1.9 %copy.12 = f32[64,2048]{1,0:T(8,128)} copy(f32[64,2048]{1,0:T(8,128)} %get-tuple-element.16) | data formatting | bytes 1048576

commit v5 on v2

--- a/solution.py
+++ b/solution.py
@@ -118,7 +118,7 @@
         return c
 
     own = [copy(src, held.at[a, at[a][0], at[a][1]], a) for a, src in enumerate((tok, tan, adj))]
-    heavy = [copy(wg_in, wg, 3), copy(wu_in, wu, 4), copy(wd_in, wd, 5)]
+    heavy = [copy(wg_in, wg, 3), copy(wu_in, wu, 4), copy(wd_in, chunk, 5)]
     turned = jnp.concatenate([ids[...].astype(F32), gates[...]], axis=1)
     for a in range(3):
         meta[a, at[a][0], at[a][1]] = turned
@@ -294,7 +294,7 @@
                         ref[:, spots2[i], :, :, cols] = value[i]
 
                 if a == 2:
-                    put(back, lax.dot_general(rows, wd[j, cols, :], NT, preferred_element_type=F32))
+                    put(back, jnp.dot(rows, wd[j, :, cols], preferred_element_type=F32))
                 else:
                     x, y = (pre, lin) if a == 0 else (dirg, diru)
                     put(x, jnp.dot(rows, wg[j, :, cols], preferred_element_type=F32))
@@ -368,11 +368,22 @@
 
     for a in range(3):
         wire.got(mk2[a][1], meta.at[a, pl.ds(0, 3)])
+    def turn_over(k):
+        if k == 0:
+            heavy[2].wait()
+
+        @pl.loop(0, 8)
+        def _(m):
+            cols = pl.ds(pl.multiple_of(m * 256, 256), 256)
+            block = chunk[k // 2, 2 * (k % 2) : 2 * (k % 2) + 2, :, :, cols].reshape(256, 256)
+            wd[k // 3, cols, 256 * (k % 3) : 256 * (k % 3) + 256] = block.T
+
     for b in (1, 2):
         for a in range(3):
             pass_on(a, ORDERS[a][1], second[a][b], *views2(a, b))
             weigh(a, 2 * b - 2)
             weigh(a, 2 * b - 1)
+            turn_over(3 * b - 3 + a)
         if b == 1:
             pack(0)
     for a in range(3):
@@ -390,8 +401,8 @@
     pack(3)
     direct(2)
     relays(2)
-    for c in heavy:
-        c.wait()
+    heavy[0].wait()
+    heavy[1].wait()
     fetch(0)
     pack(4)
     direct(3)
@@ -464,7 +475,7 @@
             pltpu.VMEM((3, 4, 4, 32, D), BF),
             pltpu.VMEM((2, D, FF), BF),
             pltpu.VMEM((2, D, FF), BF),
-            pltpu.VMEM((2, FF, D), BF),
+            pltpu.VMEM((2, D, FF), BF),
         ]
         + [pltpu.VMEM((4, 4, 4, 8, FF), F32)] * 5
         + [pltpu.VMEM((3, 2, 512, FF), BF)]
@@ -513,7 +524,7 @@
     for other in near + tall:
         pl.semaphore_signal(sem, inc=1, device_id=other, device_id_type=MESH)
     pl.semaphore_wait(sem, 22)
-    keys = [[[wire.group(), wire.group()] + [wire.take() for _ in range(6)] for _ in range(3)] for _ in range(3)]
+    keys = [[[wire.group(), wire.group()] + [wire.take() for _ in range(4)] for _ in range(3)] for _ in range(3)]
     at = [tuple(place.at[d] for d in ORDERS[a]) for a in range(3)]
     state = {"square": jnp.zeros((8, 128), F32)}
 
@@ -555,37 +566,23 @@
                 to2[side, 2:4] = hi.astype(BF)
                 wire.go(k[0], k[4], to2.at[side], in2.at[side], dim, r)
 
-    def far1(q):
+    def last(q):
         for a, _, n in PARTS[q]:
             own, in2, out1, mid1 = (parts[3 * q + a][i] for i in (1, 5, 6, 7))
             n1, dim = at[a][0], ORDERS[a][0]
             k = keys[q][a]
             wire.got(k[4], in2)
             own[...] = own[...] + (in2[0].astype(F32) + in2[1].astype(F32))
-            out1[0] = own[mod4(n1 + 2)].astype(BF)
-            wire.go(k[1], k[5], out1.at[0, pl.ds(0, 32)], mid1.at[0, pl.ds(0, 32)], dim, 1)
-            wire.go(k[1], k[6], out1.at[0, pl.ds(32, 32)], mid1.at[0, pl.ds(32, 32)], dim, 3)
-
-    def near1(q):
-        for a, _, n in PARTS[q]:
-            own, in2, out1, mid1 = (parts[3 * q + a][i] for i in (1, 5, 6, 7))
-            n1, dim = at[a][0], ORDERS[a][0]
-            k = keys[q][a]
-            for side, r in ((0, 1), (1, 3)):
-                rows = pl.ds(32 * side, 32)
-                rest = pl.ds(32 - 32 * side, 32)
-                wire.got(k[5 + side], mid1.at[0, rows])
-                s = mod4(n1 + r)
-                out1[1 + side, rows] = (own[s, rows] + mid1[0, rows].astype(F32)).astype(BF)
-                out1[1 + side, rest] = own[s, rest].astype(BF)
-                wire.go(k[1], k[7], out1.at[1 + side], mid1.at[1 + side], dim, r)
+            for by in (2, 1, 3):
+                out1[by - 1] = own[mod4(n1 + by)].astype(BF)
+                wire.go(k[1], k[5], out1.at[by - 1], mid1.at[by - 1], dim, by)
 
     def finish(q):
         for a, f0, n in PARTS[q]:
             own, mid1 = parts[3 * q + a][1], parts[3 * q + a][7]
             k = keys[q][a]
-            wire.got(k[7], mid1.at[pl.ds(1, 2)])
-            got = own[at[a][0]] + (mid1[1].astype(F32) + mid1[2].astype(F32))
+            wire.got(k[5], mid1)
+            got = own[at[a][0]] + (mid1[0].astype(F32) + mid1[1].astype(F32) + mid1[2].astype(F32))
             hvp[:, f0 : f0 + n] = got
             state["square"] += jnp.sum((got * got).reshape(8, 8, n // 128, 128), axis=(0, 2))
 
@@ -593,18 +590,15 @@
     far2(1)
     near2(0)
     far2(2)
-    far1(0)
+    last(0)
     near2(1)
-    near1(0)
     t = tan[...].astype(F32)
     low = jnp.sum((t * t).reshape(8, 8, 16, 128), axis=(0, 2))
-    far1(1)
     near2(2)
     finish(0)
-    near1(1)
-    far1(2)
+    last(1)
     finish(1)
-    near1(2)
+    last(2)
     finish(2)
 
     def share(table, value, spot, others):
@@ -620,7 +614,7 @@
     full = share(plane, (state["square"], low), y * 4 + x, near)
     full = share(line, (full[0], full[1]), place.dp * 4 + z, tall)
     top, low = jnp.sum(full[0]), jnp.sum(full[1])
-    ratio[...] = jnp.full((8, 128), top, F32) / jnp.full((8, 128), low, F32)
+    ratio[...] = jnp.full((1, 1), top, F32) / jnp.full((1, 1), low, F32)
     for q in range(3):
         for a in range(3):
             back, _, _, _, _, _, out1, _ = parts[3 * q + a]
@@ -628,7 +622,7 @@
             wire.sent(keys[q][a][1], out1)
 
 
-N_SENT, N_CAME = 18 + 2, 54 + 2
+N_SENT, N_CAME = 18 + 2, 36 + 2
 
 
 def collect(backs, grown, tan):
@@ -657,7 +651,7 @@
     ]
     return pl.pallas_call(
         collect_kernel,
-        out_shape=(jax.ShapeDtypeStruct((TOK, D), F32), jax.ShapeDtypeStruct((8, 128), F32)),
+        out_shape=(jax.ShapeDtypeStruct((TOK, D), F32), jax.ShapeDtypeStruct((1, 1), F32)),
         in_specs=[hbm] * 4 + [vmem],
         out_specs=(vmem, vmem),
         scratch_shapes=scratch,
@@ -669,6 +663,7 @@
 
 
 def local(tokens, tangent, adjoint, gates, expert_ids, w_gate, w_up, w_down):
+    w_down = w_down.reshape(3, 4, 4, 32, D)
     *backs, grown = dispatch(tokens, tangent, adjoint, expert_ids.T, gates.T, w_gate, w_up, w_down)
     backs = [b.reshape(4, 4, 64, b.shape[-1]) for b in backs]
     hvp, ratio = collect(backs, grown, tangent)

time: 182 us -> 179 us (0.984)
  Pallas kernels: 178 us -> 174 us
    pallas_call x1, Pallas kernels: 49.1 us -> 45.5 us  [collect(): pl.pallas_call(collect_kernel, out_shape=(jax.ShapeDtypeStruct((TOK, D),...]
where the time goes in v5:
time: 179 us; the launch traced here: 178 us
  Pallas kernels  174 us (97%)
  between operations  2.41 us (1%)
  local copies, waits for them, and re-layouts  1.87 us (1%)
    pallas_call x1, Pallas kernels, dispatch(): pl.pallas_call(dispatch_kernel, out_shape=(rows, rows, rows) + tuple((jax...  128 us
    pallas_call x1, Pallas kernels, collect(): pl.pallas_call(collect_kernel, out_shape=(jax.ShapeDtypeStruct((TOK, D),...  45.5 us

profile of v5, /device:TPU:1, one launch (start us, length us, event | category | flops | bytes accessed | tf_op | source)
XLA Modules:
  0.0 178.3 jit_solution(1321620097561387345)
XLA Ops:
  0.6 128.5 %dispatch.1 = (bf16[2,4,4,32,2048]{4,3,2,1,0:T(8,128)(2,1)}, bf16[2,4,4,32,2048]{4,3,2,1,0:T(8,128)(2,1)}, bf16[2,4,4,32,2048]{4,3,2,1,0:T(8,128)(2,1)}, bf16[4,...) custom-call(bf16[64,2048]{1,0:T(8,128)(2,1)} %tok.1, ...), custom_call_target="tpu_custom_call" | custom-call | tf_op jit(solution)/shard_map/dispatch/pallas_call | solution.py:463
  129.1 45.5 %collect.1 = (f32[64,2048]{1,0:T(8,128)}, f32[1,1]{1,0:T(1,128)}) custom-call(bf16[4,4,64,768]{3,2,1,0:T(8,128)(2,1)} %bitcast.8, bf16[4,4,64,640]{3,2,1,0:T(8,128)(2,1)} %bitcast.9, bf16[4,4,64,640]{3,2,1,0:T(8,128)(2,1)} %bitcast.10, bf16[3,4,2,256,256]{4,3,2,1,0:T(8,128)(2,1)} %get-tuple-element.11.grown_in, bf16[64,2048]{1,0:T(8,128)(2,1)} %tan.3), custom_call_target="tpu_custom_call" | custom-call | tf_op jit(solution)/shard_map/collect/pallas_call | solution.py:652
  174.6 1.9 %copy.12 = f32[64,2048]{1,0:T(8,128)} copy(f32[64,2048]{1,0:T(8,128)} %get-tuple-element.16) | data formatting | bytes 1048576

commit v6 on v5

--- a/solution.py
+++ b/solution.py
@@ -422,17 +422,17 @@
     pack(7)
     direct(6)
     relays(6)
+    fetch(4)
+    direct(7)
     mix()
-    direct(7)
     relays(7)
-    fetch(4)
     fetch(5)
     layer(4, (0, 1, 2))
+    fetch(6)
     reply(0)
-    fetch(6)
     fetch(7)
+    layer(6, (0, 1, 2))
     replays(0)
-    layer(6, (0, 1, 2))
     mix()
     reply(1)
     replays(1)

time: 179 us -> 175 us (0.978)
  Pallas kernels: 174 us -> 171 us
    pallas_call x1, Pallas kernels: 45.5 us -> 43.3 us  [collect(): pl.pallas_call(collect_kernel, out_shape=(jax.ShapeDtypeStruct((TOK, D),...]
where the time goes in v6:
time: 175 us
  Pallas kernels  171 us (98%)
  between operations  2.41 us (1%)
  local copies, waits for them, and re-layouts  1.87 us (1%)
    pallas_call x1, Pallas kernels, dispatch(): pl.pallas_call(dispatch_kernel, out_shape=(rows, rows, rows) + tuple((jax...  127 us
    pallas_call x1, Pallas kernels, collect(): pl.pallas_call(collect_kernel, out_shape=(jax.ShapeDtypeStruct((TOK, D),...  43.3 us

profile of v6, /device:TPU:1, one launch (start us, length us, event | category | flops | bytes accessed | tf_op | source)
XLA Modules:
  0.0 175.1 jit_solution(6301108129485693215)
XLA Ops:
  0.6 127.4 %dispatch.1 = (bf16[2,4,4,32,2048]{4,3,2,1,0:T(8,128)(2,1)}, bf16[2,4,4,32,2048]{4,3,2,1,0:T(8,128)(2,1)}, bf16[2,4,4,32,2048]{4,3,2,1,0:T(8,128)(2,1)}, bf16[4,...) custom-call(bf16[64,2048]{1,0:T(8,128)(2,1)} %tok.1, ...), custom_call_target="tpu_custom_call" | custom-call | tf_op jit(solution)/shard_map/dispatch/pallas_call | solution.py:463
  128.1 43.3 %collect.1 = (f32[64,2048]{1,0:T(8,128)}, f32[1,1]{1,0:T(1,128)}) custom-call(bf16[4,4,64,768]{3,2,1,0:T(8,128)(2,1)} %bitcast.8, bf16[4,4,64,640]{3,2,1,0:T(8,128)(2,1)} %bitcast.9, bf16[4,4,64,640]{3,2,1,0:T(8,128)(2,1)} %bitcast.10, bf16[3,4,2,256,256]{4,3,2,1,0:T(8,128)(2,1)} %get-tuple-element.11.grown_in, bf16[64,2048]{1,0:T(8,128)(2,1)} %tan.3), custom_call_target="tpu_custom_call" | custom-call | tf_op jit(solution)/shard_map/collect/pallas_call | solution.py:652
  171.4 1.9 %copy.12 = f32[64,2048]{1,0:T(8,128)} copy(f32[64,2048]{1,0:T(8,128)} %get-tuple-element.16) | data formatting | bytes 1048576

commit v7 on v6

--- a/solution.py
+++ b/solution.py
@@ -424,8 +424,8 @@
     relays(6)
     fetch(4)
     direct(7)
+    relays(7)
     mix()
-    relays(7)
     fetch(5)
     layer(4, (0, 1, 2))
     fetch(6)

time: 175 us -> 177 us (1.011)
  Pallas kernels: 171 us -> 173 us
    pallas_call x1, Pallas kernels: 127 us -> 130 us  [dispatch(): pl.pallas_call(dispatch_kernel, out_shape=(rows, rows, rows) + tuple((jax...]
where the time goes in v7:
time: 177 us
  Pallas kernels  173 us (98%)
  between operations  2.41 us (1%)
  local copies, waits for them, and re-layouts  1.87 us (1%)
    pallas_call x1, Pallas kernels, dispatch(): pl.pallas_call(dispatch_kernel, out_shape=(rows, rows, rows) + tuple((jax...  130 us
    pallas_call x1, Pallas kernels, collect(): pl.pallas_call(collect_kernel, out_shape=(jax.ShapeDtypeStruct((TOK, D),...  43.3 us

profile of v7, /device:TPU:1, one launch (start us, length us, event | category | flops | bytes accessed | tf_op | source)
XLA Modules:
  0.0 177.2 jit_solution(12178122085015358903)
XLA Ops:
  0.6 129.6 %dispatch.1 = (bf16[2,4,4,32,2048]{4,3,2,1,0:T(8,128)(2,1)}, bf16[2,4,4,32,2048]{4,3,2,1,0:T(8,128)(2,1)}, bf16[2,4,4,32,2048]{4,3,2,1,0:T(8,128)(2,1)}, bf16[4,...) custom-call(bf16[64,2048]{1,0:T(8,128)(2,1)} %tok.1, ...), custom_call_target="tpu_custom_call" | custom-call | tf_op jit(solution)/shard_map/dispatch/pallas_call | solution.py:463
  130.2 43.3 %collect.1 = (f32[64,2048]{1,0:T(8,128)}, f32[1,1]{1,0:T(1,128)}) custom-call(bf16[4,4,64,768]{3,2,1,0:T(8,128)(2,1)} %bitcast.8, bf16[4,4,64,640]{3,2,1,0:T(8,128)(2,1)} %bitcast.9, bf16[4,4,64,640]{3,2,1,0:T(8,128)(2,1)} %bitcast.10, bf16[3,4,2,256,256]{4,3,2,1,0:T(8,128)(2,1)} %get-tuple-element.11.grown_in, bf16[64,2048]{1,0:T(8,128)(2,1)} %tan.3), custom_call_target="tpu_custom_call" | custom-call | tf_op jit(solution)/shard_map/collect/pallas_call | solution.py:652
  173.5 1.9 %copy.12 = f32[64,2048]{1,0:T(8,128)} copy(f32[64,2048]{1,0:T(8,128)} %get-tuple-element.16) | data formatting | bytes 1048576
